TPU v7x, 768 devices: a whole 4x8x12 slice. The times are simulated.
768 devices in a mesh: dom: 192 (over z, y, core), sub: 4 (over x).
Axes of the slice: x: 4, y: 8, z: 12, core: 2. Of those that a mesh axis runs over, the one named last changes fastest.
Arguments:
- wavefield: float32 [9, 35, 344064], P(None, None, ('dom', 'sub')), may hold values from -6 to 6
- material: float32 [3, 344064], P(None, ('dom', 'sub')), may hold values from 0.5 to 4
- geometry: float32 [3, 3, 344064], P(None, None, ('dom', 'sub')), may hold values from -4 to 4
- face_scale: float32 [4, 344064], P(None, ('dom', 'sub')), may hold values from 0.5 to 2
- derivative: float32 [3, 35, 35], replicated, may hold values from -1 to 1
- lift_matrix: float32 [35, 60], replicated, may hold values from -0.75 to 0.75
- neighbour: int32 [4, 344064], P(None, ('dom', 'sub')), may hold values from 0 to 1343, as said below
- orient: int32 [4, 344064], P(None, ('dom', 'sub')), may hold values from 0 to 2
- halo_faces: int32 [2, 172032], P(None, ('dom', 'sub')), may hold values from 0 to 1023, as said below
- interface_send: int32 [2, 3, 24576], P(None, None, ('dom', 'sub')), may hold values from 0 to 1023, as said below
Outputs:
- new_wavefield: float32 [9, 35, 344064], P(None, None, ('dom', 'sub'))
Inputs may be any that keep to these rules, and one draw needn't show every extreme that they name: `neighbour`: for a face of a partition's cluster with E elements, the entry names a column of that cluster's table: 0 .. 4 * E - 1 its own faces, then E / 2 from the partition before, E / 2 from the one after, 32 of the first and 32 of the second buffer; each of the last E + 64 columns is named by exactly one face. `halo_faces`: within a partition's block, the fine segment names faces below 256, the middle below 512, the coarse below 1024. `interface_send`: entries name faces of the sending cluster: for side 0 the fine, fine, middle cluster of pairs 0, 1, 2; for side 1 the middle, coarse, coarse cluster; each below 4 times that cluster's element count.
All inputs are finite; a program needn't handle non-finite values.
Results may differ from a plain program's by a relative error of at most 0.0003.
Values sent between devices are 32-bit elements; how exact they have to be, the bound alone decides.
A program may use at most 128 MiB of HBM per device.

v0:
```python
import jax
import jax.numpy as jnp
import numpy as np
from jax import lax
from jax.sharding import PartitionSpec as P

EF = 64
EM = 128
EC = 256


PENALTY = 0.5
COARSE_STEP = 0.1
highest = lax.Precision.HIGHEST


def padded(block, sides, width):
    for axis, dim in sides:
        count = lax.axis_size(axis)
        forward = [(i, i + 1) for i in range(count - 1)]
        backward = [(target, source) for source, target in forward]
        low = lax.ppermute(
            lax.slice_in_dim(block, block.shape[dim] - width, None, axis=dim), axis, forward
        )
        high = lax.ppermute(lax.slice_in_dim(block, 0, width, axis=dim), axis, backward)
        block = jnp.concatenate([low, block, high], axis=dim)
    return block


def face_tables():
    lattice = [
        (corner_a, corner_b, corner_c, 4 - corner_a - corner_b - corner_c)
        for corner_a in range(5)
        for corner_b in range(5 - corner_a)
        for corner_c in range(5 - corner_a - corner_b)
    ]
    face_rows = np.array(
        [
            [number for number, coords in enumerate(lattice) if coords[face_id] == 0]
            for face_id in range(4)
        ],
        np.int32,
    )
    triangle = [coords[1:] for coords in lattice if coords[0] == 0]
    position = {coords: number for number, coords in enumerate(triangle)}

    def turned(coords, times_turn):
        flipped = (coords[1], coords[0], coords[2])
        for repeat in range(times_turn):
            flipped = (flipped[1], flipped[2], flipped[0])
        return flipped

    orders = np.array(
        [[position[turned(coords, times_turn)] for coords in triangle] for times_turn in range(3)],
        np.int32,
    )
    return (face_rows, orders)


def face_traces(element_state, face_rows):
    elem_count = element_state.shape[2]
    picked = element_state[:, face_rows.reshape(-1), :].reshape(9, 4, 15, elem_count)
    return picked.transpose(0, 2, 1, 3).reshape(135, 4 * elem_count)


def element_rate(
    element_state,
    material,
    geometry,
    face_scale,
    trace_table,
    neighbour,
    orient,
    derivative,
    lift_matrix,
    face_rows,
    orders,
):
    elem_count = element_state.shape[2]
    along_ref = jnp.einsum("kmn,qne->kqme", derivative, element_state, precision=highest)
    physical = jnp.einsum("ike,kqme->iqme", geometry, along_ref, precision=highest)
    density = material[0]
    lame_first = material[1]
    shear_mod = material[2]
    voigt_index = ((3, 8, 7), (8, 4, 6), (7, 6, 5))
    rate_list = []
    for direction in range(3):
        rate_list.append(
            (
                physical[0, voigt_index[direction][0]]
                + physical[1, voigt_index[direction][1]]
                + physical[2, voigt_index[direction][2]]
            )
            / density
        )
    divergence = physical[0, 0] + physical[1, 1] + physical[2, 2]
    for direction in range(3):
        rate_list.append(lame_first * divergence + 2.0 * shear_mod * physical[direction, direction])
    rate_list.append(shear_mod * (physical[1, 2] + physical[2, 1]))
    rate_list.append(shear_mod * (physical[0, 2] + physical[2, 0]))
    rate_list.append(shear_mod * (physical[0, 1] + physical[1, 0]))
    volume = jnp.stack(rate_list)
    own_side = face_traces(element_state, face_rows).reshape(9, 15, 4 * elem_count)
    columns = trace_table.shape[1]
    flat_table = trace_table.reshape(9, 15 * columns)
    node_order = jnp.take(jnp.asarray(orders), orient.reshape(-1), axis=0).transpose(1, 0)
    flat_index = (node_order * columns + neighbour.reshape(-1)[None, :]).astype(jnp.int32)
    aligned = jnp.take(flat_table, flat_index.reshape(-1), axis=1).reshape(9, 15, 4 * elem_count)
    face_jump = (aligned - own_side) * (PENALTY * face_scale.reshape(-1))
    face_jump = (
        face_jump.reshape(9, 15, 4, elem_count).transpose(0, 2, 1, 3).reshape(9, 60, elem_count)
    )
    surface = jnp.einsum("mn,qne->qme", lift_matrix, face_jump, precision=highest)
    return volume + surface


def on_device(
    wavefield,
    material,
    geometry,
    face_scale,
    derivative,
    lift_matrix,
    neighbour,
    orient,
    halo_faces,
    interface_send,
):
    face_rows, orders = face_tables()
    width_x = interface_send.shape[2]
    elem_cuts = (0, EF, EF + EM, EF + EM + EC)
    halo_cuts = (0, EF // 2, EF // 2 + EM // 2, (EF + EM + EC) // 2)

    def part_of(array, cluster):
        return array[..., elem_cuts[cluster] : elem_cuts[cluster + 1]]

    def halo_send(own_side, cluster):
        columns = halo_faces[:, halo_cuts[cluster] : halo_cuts[cluster + 1]]
        return jnp.stack(
            [jnp.take(own_side, columns[0], axis=1), jnp.take(own_side, columns[1], axis=1)]
        )

    def traded(own_side, cluster):
        return padded(halo_send(own_side, cluster), ((("dom", "sub"), 0),), 1)

    def update(field_block, cluster, own_side, received, extras, step_size):
        trace_table = jnp.concatenate([own_side, received[0], received[3]] + extras, axis=1)
        tendency = element_rate(
            field_block,
            part_of(material, cluster),
            part_of(geometry, cluster),
            part_of(face_scale, cluster),
            trace_table,
            part_of(neighbour, cluster),
            part_of(orient, cluster),
            derivative,
            lift_matrix,
            face_rows,
            orders,
        )
        return field_block + step_size * tendency

    fields = [part_of(wavefield, cluster) for cluster in range(3)]
    start_own = [face_traces(fields[cluster], face_rows) for cluster in range(3)]

    def received_for(own_side, cluster):
        return traded(own_side, cluster)

    coarse_sends = (
        jnp.take(start_own[1], interface_send[1, 0], axis=1),
        jnp.take(start_own[2], interface_send[1, 1], axis=1),
        jnp.take(start_own[2], interface_send[1, 2], axis=1),
    )
    from_mid_fm, from_slow_fc, from_slow_mc = (
        lax.all_to_all(coarse_sends[0], "sub", split_axis=1, concat_axis=1, tiled=True),
        lax.all_to_all(coarse_sends[1], "sub", split_axis=1, concat_axis=1, tiled=True),
        lax.all_to_all(coarse_sends[2], "sub", split_axis=1, concat_axis=1, tiled=True),
    )
    zero_buffer = jnp.zeros((135, width_x), jnp.float32)
    halves = [zero_buffer, zero_buffer]
    whole_fc = zero_buffer
    fast_state = fields[0]
    for substep in range(4):
        own_side = start_own[0] if substep == 0 else face_traces(fast_state, face_rows)
        halves[substep // 2] = halves[substep // 2] + 0.5 * jnp.take(
            own_side, interface_send[0, 0], axis=1
        )
        whole_fc = whole_fc + 0.25 * jnp.take(own_side, interface_send[0, 1], axis=1)
        fast_state = update(
            fast_state,
            0,
            own_side,
            received_for(own_side, 0),
            [from_mid_fm, from_slow_fc],
            COARSE_STEP / 4,
        )
    recv_first, recv_second, recv_fc = (
        lax.all_to_all(halves[0], "sub", split_axis=1, concat_axis=1, tiled=True),
        lax.all_to_all(halves[1], "sub", split_axis=1, concat_axis=1, tiled=True),
        lax.all_to_all(whole_fc, "sub", split_axis=1, concat_axis=1, tiled=True),
    )
    mid_sum = zero_buffer
    mid_state = fields[1]
    for substep in range(2):
        own_side = start_own[1] if substep == 0 else face_traces(mid_state, face_rows)
        mid_sum = mid_sum + 0.5 * jnp.take(own_side, interface_send[0, 2], axis=1)
        mid_state = update(
            mid_state,
            1,
            own_side,
            received_for(own_side, 1),
            [(recv_first, recv_second)[substep], from_slow_mc],
            COARSE_STEP / 2,
        )
    recv_mc = lax.all_to_all(mid_sum, "sub", split_axis=1, concat_axis=1, tiled=True)
    slow_state = update(
        fields[2], 2, start_own[2], received_for(start_own[2], 2), [recv_fc, recv_mc], COARSE_STEP
    )
    return jnp.concatenate([fast_state, mid_state, slow_state], axis=2)


def solution(mesh):
    placed = (
        P(None, None, ("dom", "sub")),
        P(None, ("dom", "sub")),
        P(None, None, ("dom", "sub")),
        P(None, ("dom", "sub")),
        P(),
        P(),
        P(None, ("dom", "sub")),
        P(None, ("dom", "sub")),
        P(None, ("dom", "sub")),
        P(None, None, ("dom", "sub")),
    )
    return jax.shard_map(
        on_device,
        mesh=mesh,
        in_specs=placed,
        out_specs=P(None, None, ("dom", "sub")),
        check_vma=False,
    )
```

profile of v0, /device:TPU:512, one launch (start us, length us, event | category | flops | bytes accessed | tf_op | source)
XLA Modules:
  0.0 477.1 jit_solution(945794672778133462)
XLA Ops:
  6.4 8.2 %collective-permute-start.1 = (f32[1,135,32]{1,2,0:T(8,128)}, f32[1,135,32]{1,2,0:T(8,128)}, u32[]{:S(2)}, u32[]{:S(2)}) collective-permute-start(f32[1,135,32]{1,2,0:T(8,128)} %select_bitcast_fusion.15), channel_id=1, source_target_pairs={{1,0},{2,1},{3,2},{4,3},{5,4},{6,5},{7,6},{8,7},{9,8},{10,9},{11,1... | collective-permute-start | bytes 51848 | tf_op jit(solution)/shard_map/ppermute | solution.py:25
  21.6 3.9 all-to-all-start
  27.0 9.1 %collective-permute-start.9 = (f32[1,135,64]{1,2,0:T(8,128)}, f32[1,135,64]{1,2,0:T(8,128)}, u32[]{:S(2)}, u32[]{:S(2)}) collective-permute-start(f32[1,135,64]{1,2,0:T(8,128)} %select_bitcast_fusion.4), channel_id=1, source_target_pairs={{1,0},{2,1},{3,2},{4,3},{5,4},{6,5},{7,6},{8,7},{9,8},{10,9},{11,1... | collective-permute-start | bytes 103688 | tf_op jit(solution)/shard_map/ppermute | solution.py:25
  43.9 9.3 %collective-permute-start.13 = (f32[1,135,128]{1,2,0:T(8,128)}, f32[1,135,128]{1,2,0:T(8,128)}, u32[]{:S(2)}, u32[]{:S(2)}) collective-permute-start(f32[1,135,128]{1,2,0:T(8,128)} %select_bitcast_fusion), channel_id=1, source_target_pairs={{1,0},{2,1},{3,2},{4,3},{5,4},{6,5},{7,6},{8,7},{9,8},{10,9},{11,1... | collective-permute-start | bytes 207368 | tf_op jit(solution)/shard_map/ppermute | solution.py:25
  61.8 2.8 gather_fusion.7
  81.3 3.4 fusion.54
  92.3 5.7 %fusion.38 = f32[128,9,35,3]{2,3,1,0:T(4,128)} fusion(f32[3,9,35,128]{2,0,1,3:T(4,128)S(1)} %copy.347, f32[3,3,128]{1,0,2:T(4,128)S(1)} %copy.422), kind=kOutput, calls=%fused_computation.114 | convolution fusion | flops 4354560 | bytes 972288 | tf_op jit(solution)/shard_map/ike,kqme->iqme/dot_general | solution.py:81
  100.5 4.2 copy.376
  104.8 12.7 %fusion.168 = f32[256,9,35,3]{2,3,1,0:T(4,128)} fusion(f32[3,9,35,256]{2,0,1,3:T(4,128)} %copy.376, f32[3,3,256,1]{1,0,3,2:T(4,128)S(1)} %copy-done.33), kind=kOutput, calls=%fused_computation.494 | convolution fusion | flops 8709120 | bytes 1944576 | tf_op jit(solution)/shard_map/ike,kqme->iqme/dot_general | solution.py:81
  117.5 3.9 copy.378
  124.6 3.3 all-to-all-start.1
  127.9 5.4 %all-to-all-done.1 = f32[135,4,8]{0,2,1:T(8,128)S(1)} async-done(((f32[135,4,8]{0,2,1:T(8,128)}), f32[135,4,8]{0,2,1:T(8,128)S(1)}, u32[]{:S(2)}, u32[]{:S(2)}) %all-to-all-start.1) | async-done | bytes 17312 | tf_op jit(solution)/shard_map/all_to_all | solution.py:176
  133.3 3.3 all-to-all-start.3
  146.6 7.9 %gather_fusion.14 = f32[3840,9]{1,0:T(8,128)} fusion(f32[9,5760]{0,1:T(8,128)S(1)} %copy.305, s32[4096]{0:T(1024)S(1)} %pad_clamp_fusion.1), kind=kCustom, calls=%fused_computation.4.clone | custom fusion | bytes 291840 | tf_op jit(solution)/shard_map/jit(_take)/gather | solution.py:108
  154.4 3.5 broadcast_select_fusion.5
  167.2 4.1 collective-permute-start.2
  171.9 2.3 fusion.52
  180.2 2.5 copy.318
  182.7 7.9 %gather_fusion.17 = f32[3840,9]{1,0:T(8,128)} fusion(f32[9,5760]{0,1:T(8,128)S(1)} %copy.318, s32[4096]{0:T(1024)S(1)} %pad_clamp_fusion.1), kind=kCustom, calls=%fused_computation.27.clone | custom fusion | bytes 291840 | tf_op jit(solution)/shard_map/jit(_take)/gather | solution.py:108
  190.6 3.5 broadcast_select_fusion.4
  201.2 7.1 %collective-permute-start.5 = (f32[1,135,32]{1,2,0:T(8,128)}, f32[1,135,32]{1,2,0:T(8,128)}, u32[]{:S(2)}, u32[]{:S(2)}) collective-permute-start(f32[1,135,32]{1,2,0:T(8,128)} %select_bitcast_fusion.9), channel_id=1, source_target_pairs={{1,0},{2,1},{3,2},{4,3},{5,4},{6,5},{7,6},{8,7},{9,8},{10,9},{11,1... | collective-permute-start | bytes 51848 | tf_op jit(solution)/shard_map/ppermute | solution.py:25
  210.8 2.3 fusion.50
  224.3 2.5 copy.331
  226.8 7.9 %gather_fusion.20 = f32[3840,9]{1,0:T(8,128)} fusion(f32[9,5760]{0,1:T(8,128)S(1)} %copy.331, s32[4096]{0:T(1024)S(1)} %pad_clamp_fusion.1), kind=kCustom, calls=%fused_computation.28.clone | custom fusion | bytes 291840 | tf_op jit(solution)/shard_map/jit(_take)/gather | solution.py:108
  234.7 3.5 broadcast_select_fusion.3
  246.2 4.6 all-to-all-start.2
  252.2 9.6 %collective-permute-start.7 = (f32[1,135,32]{1,2,0:T(8,128)}, f32[1,135,32]{1,2,0:T(8,128)}, u32[]{:S(2)}, u32[]{:S(2)}) collective-permute-start(f32[1,135,32]{1,2,0:T(8,128)} %select_bitcast_fusion.7), channel_id=1, source_target_pairs={{1,0},{2,1},{3,2},{4,3},{5,4},{6,5},{7,6},{8,7},{9,8},{10,9},{11,1... | collective-permute-start | bytes 51848 | tf_op jit(solution)/shard_map/ppermute | solution.py:25
  267.9 3.9 all-to-all-start.4
  274.0 3.3 copy.359
  277.3 17.4 %gather_fusion.30 = f32[7680,9]{1,0:T(8,128)} fusion(f32[9,10560]{0,1:T(8,128)} %copy.359, s32[8192]{0:T(1024)S(1)} %copy-done.62), kind=kCustom, calls=%fused_computation.7.clone | custom fusion | bytes 583680 | tf_op jit(solution)/shard_map/jit(_take)/gather | solution.py:108
  294.7 7.2 %broadcast_select_fusion.1 = f32[7680,9]{1,0:T(8,128)} fusion(f32[7680,9]{1,0:T(8,128)} %gather_fusion.30, pred[7680]{0:T(1024)(128)(4,1)S(1)} %copy-done.77), kind=kLoop, calls=%fused_computation.45 | loop fusion | flops 69120 | bytes 560640 | tf_op jit(solution)/shard_map/jit(_take)/select_n | solution.py:108
  301.9 2.9 copy.360
  313.3 9.4 %collective-permute-start.11 = (f32[1,135,64]{1,2,0:T(8,128)}, f32[1,135,64]{1,2,0:T(8,128)}, u32[]{:S(2)}, u32[]{:S(2)}) collective-permute-start(f32[1,135,64]{1,2,0:T(8,128)} %select_bitcast_fusion.2), channel_id=1, source_target_pairs={{1,0},{2,1},{3,2},{4,3},{5,4},{6,5},{7,6},{8,7},{9,8},{10,9},{11,1... | collective-permute-start | bytes 103688 | tf_op jit(solution)/shard_map/ppermute | solution.py:25
  325.0 5.7 %fusion.36 = f32[128,9,35,3]{2,3,1,0:T(4,128)} fusion(f32[3,9,35,128]{2,0,1,3:T(4,128)S(1)} %copy.361, f32[3,3,128]{1,0,2:T(4,128)S(1)} %copy-done.32), kind=kOutput, calls=%fused_computation.112 | convolution fusion | flops 4354560 | bytes 972288 | tf_op jit(solution)/shard_map/ike,kqme->iqme/dot_general | solution.py:81
  333.8 3.3 all-to-all-start.5
  338.6 3.9 all-to-all-done.5
  343.2 3.9 all-to-all-start.6
  347.1 3.9 collective-permute-start.10
  353.7 2.5 copy.344
  356.2 7.9 %gather_fusion.23 = f32[3840,9]{1,0:T(8,128)} fusion(f32[9,5760]{0,1:T(8,128)S(1)} %copy.344, s32[4096]{0:T(1024)S(1)} %pad_clamp_fusion.1), kind=kCustom, calls=%fused_computation.29.clone | custom fusion | bytes 291840 | tf_op jit(solution)/shard_map/jit(_take)/gather | solution.py:108
  364.1 3.5 broadcast_select_fusion.2
  373.3 5.7 %copy.393 = f32[9,20160]{0,1:T(8,128)} copy(f32[9,20160]{1,0:T(8,128)S(1)} %reshape.4142) | data formatting | bytes 1451520 | tf_op jit(solution)/shard_map/reshape | solution.py:105
  378.9 55.1 %gather_fusion.8 = f32[15360,9]{1,0:T(8,128)} fusion(f32[9,20160]{0,1:T(8,128)} %copy.393, s32[15360]{0:T(1024)S(1)} %copy-done.67), kind=kCustom, calls=%fused_computation.43 | custom fusion | bytes 1167360 | tf_op jit(solution)/shard_map/jit(_take)/gather | solution.py:108
  434.0 5.2 %copy.394 = f32[9,15,4,256]{3,1,2,0:T(8,128)S(1)} copy(f32[9,15,4,256]{0,3,2,1:T(8,128)} %bitcast.926) | data formatting | bytes 1105920 | tf_op jit(solution)/shard_map/jit(_take)/gather | solution.py:108
  444.2 3.3 copy.374
  447.5 17.4 %gather_fusion.35 = f32[7680,9]{1,0:T(8,128)} fusion(f32[9,10560]{0,1:T(8,128)} %copy.374, s32[8192]{0:T(1024)S(1)} %copy-done.63), kind=kCustom, calls=%fused_computation.33.clone | custom fusion | bytes 583680 | tf_op jit(solution)/shard_map/jit(_take)/gather | solution.py:108
  464.9 7.2 %broadcast_select_fusion = f32[7680,9]{1,0:T(8,128)} fusion(f32[7680,9]{1,0:T(8,128)} %gather_fusion.35, pred[7680]{0:T(1024)(128)(4,1)S(1)} %copy-done.77), kind=kLoop, calls=%fused_computation.44 | loop fusion | flops 69120 | bytes 560640 | tf_op jit(solution)/shard_map/jit(_take)/select_n | solution.py:108
  472.1 2.9 copy.375
  (613 shorter events, 153.7 us)
Async XLA Ops:
  0.0 66.9 %copy-start = (f32[3,35,35]{2,1,0:T(8,128)S(1)}, f32[3,35,35]{2,1,0:T(8,128)}, u32[]{:S(2)}) copy-start(f32[3,35,35]{2,1,0:T(8,128)} %param.61) | copy-start | bytes 44104
  1.5 13.7 %copy-start.102 = (pred[32]{0:T(512)(128)(4,1)}, pred[32]{0:T(512)(128)(4,1)S(1)}, u32[]{:S(2)}) copy-start(pred[32]{0:T(512)(128)(4,1)S(1)} %get-tuple-element.40) | copy-start | bytes 100
  1.5 13.7 %copy-start.106 = (pred[32]{0:T(512)(128)(4,1)}, pred[32]{0:T(512)(128)(4,1)S(1)}, u32[]{:S(2)}) copy-start(pred[32]{0:T(512)(128)(4,1)S(1)} %get-tuple-element.78) | copy-start | bytes 100
  1.6 13.6 %copy-start.111 = (s32[1024]{0:T(1024)}, s32[1024]{0:T(1024)S(1)}, u32[]{:S(2)}) copy-start(s32[1024]{0:T(1024)S(1)} %pad_clamp_fusion.13) | copy-start | bytes 12292
  2.5 15.3 %copy-start.4 = (f32[9,35,448]{2,1,0:T(8,128)S(1)}, f32[9,35,448]{2,1,0:T(8,128)}, u32[]{:S(2)}) copy-start(f32[9,35,448]{2,1,0:T(8,128)} %param.57) | copy-start | bytes 1693444
  3.3 37.1 %copy-start.97 = (s32[1024]{0:T(1024)}, s32[1024]{0:T(1024)S(1)}, u32[]{:S(2)}) copy-start(s32[1024]{0:T(1024)S(1)} %get-tuple-element.85) | copy-start | bytes 12292
  3.3 14.7 %copy-start.129 = (s32[2,3,32]{2,0,1:T(2,128)S(1)}, s32[2,3,32]{2,0,1:T(2,128)}, u32[]{:S(2)}) copy-start(s32[2,3,32]{2,0,1:T(2,128)} %param.66) | copy-start | bytes 2308
  4.9 13.7 %copy-start.42 = (f32[135,256]{1,0:T(8,128)}, f32[135,256]{1,0:T(8,128)S(1)}, u32[]{:S(2)}) copy-start(f32[135,256]{1,0:T(8,128)S(1)} %reshape.4098) | copy-start | bytes 414724
  6.4 136.3 %collective-permute-start.1 = (f32[1,135,32]{1,2,0:T(8,128)}, f32[1,135,32]{1,2,0:T(8,128)}, u32[]{:S(2)}, u32[]{:S(2)}) collective-permute-start(f32[1,135,32]{1,2,0:T(8,128)} %select_bitcast_fusion.15), channel_id=1, source_target_pairs={{1,0},{2,1},{3,2},{4,3},{5,4},{6,5},{7,6},{8,7},{9,8},{10,9},{11,1... | collective-permute-start | bytes 51848 | tf_op jit(solution)/shard_map/ppermute | solution.py:25
  15.9 127.6 %collective-permute-start = (f32[1,135,32]{1,2,0:T(8,128)}, f32[1,135,32]{1,2,0:T(8,128)}, u32[]{:S(2)}, u32[]{:S(2)}) collective-permute-start(f32[1,135,32]{1,2,0:T(8,128)} %select_bitcast_fusion.16), channel_id=1, source_target_pairs={{0,1},{1,2},{2,3},{3,4},{4,5},{5,6},{6,7},{7,8},{8,9},{9,10},{10,1... | collective-permute-start | bytes 51848 | tf_op jit(solution)/shard_map/ppermute | solution.py:22
  20.1 20.1 %copy-start.27 = (f32[17,8,4,128]{3,1,2,0:T(8,128)}, f32[17,8,4,128]{3,1,2,0:T(8,128)S(1)}, u32[]{:S(2)}) copy-start(f32[17,8,4,128]{3,1,2,0:T(8,128)S(1)} %copy.423) | copy-start | bytes 835588
  21.6 102.9 %all-to-all-start = ((f32[135,4,8]{0,2,1:T(8,128)}), f32[135,4,8]{0,2,1:T(8,128)}, u32[]{:S(2)}, u32[]{:S(2)}) async-start(f32[135,4,8]{0,2,1:T(8,128)} %select_bitcast_fusion.14), calls=%async_computation | async-start | bytes 65536 | tf_op jit(solution)/shard_map/all_to_all | solution.py:175
  25.6 15.5 %copy-start.124 = (pred[64]{0:T(512)(128)(4,1)}, pred[64]{0:T(512)(128)(4,1)S(1)}, u32[]{:S(2)}) copy-start(pred[64]{0:T(512)(128)(4,1)S(1)} %get-tuple-element.76) | copy-start | bytes 196
  25.6 15.5 %copy-start.117 = (s32[1024]{0:T(1024)}, s32[1024]{0:T(1024)S(1)}, u32[]{:S(2)}) copy-start(s32[1024]{0:T(1024)S(1)} %pad_clamp_fusion.8) | copy-start | bytes 12292
  27.0 189.3 %collective-permute-start.9 = (f32[1,135,64]{1,2,0:T(8,128)}, f32[1,135,64]{1,2,0:T(8,128)}, u32[]{:S(2)}, u32[]{:S(2)}) collective-permute-start(f32[1,135,64]{1,2,0:T(8,128)} %select_bitcast_fusion.4), channel_id=1, source_target_pairs={{1,0},{2,1},{3,2},{4,3},{5,4},{6,5},{7,6},{8,7},{9,8},{10,9},{11,1... | collective-permute-start | bytes 103688 | tf_op jit(solution)/shard_map/ppermute | solution.py:25
  37.5 182.5 %collective-permute-start.8 = (f32[1,135,64]{1,2,0:T(8,128)}, f32[1,135,64]{1,2,0:T(8,128)}, u32[]{:S(2)}, u32[]{:S(2)}) collective-permute-start(f32[1,135,64]{1,2,0:T(8,128)} %select_bitcast_fusion.5), channel_id=1, source_target_pairs={{0,1},{1,2},{2,3},{3,4},{4,5},{5,6},{6,7},{7,8},{8,9},{9,10},{10,1... | collective-permute-start | bytes 103688 | tf_op jit(solution)/shard_map/ppermute | solution.py:22
  41.6 15.6 %copy-start.90 = (f32[3,3,448]{2,1,0:T(4,128)S(1)}, f32[3,3,448]{2,1,0:T(4,128)}, u32[]{:S(2)}) copy-start(f32[3,3,448]{2,1,0:T(4,128)} %param.59) | copy-start | bytes 48388
  41.6 17.0 %slice-start.2 = ((s32[4,448]{1,0:T(4,128)}), s32[4,64]{1,0:T(4,128)S(1)}, s32[]{:S(2)}) async-start(s32[4,448]{1,0:T(4,128)} %param.63), calls=%async_computation.9 | async-start | bytes 4096 | tf_op jit(solution)/shard_map/slice | solution.py:135
  41.7 17.1 %copy-start.1 = (s32[3,15]{1,0:T(4,128)S(1)}, s32[3,15]{1,0:T(4,128)}, u32[]{:S(2)}) copy-start(s32[3,15]{1,0:T(4,128)} %constant.118.clone) | copy-start | bytes 544
  42.0 17.6 %copy-start.6 = (f32[17,8,4,256]{3,1,2,0:T(8,128)}, f32[17,8,4,256]{3,1,2,0:T(8,128)S(1)}, u32[]{:S(2)}) copy-start(f32[17,8,4,256]{3,1,2,0:T(8,128)S(1)} %copy.424) | copy-start | bytes 1671172
  43.9 325.9 %collective-permute-start.13 = (f32[1,135,128]{1,2,0:T(8,128)}, f32[1,135,128]{1,2,0:T(8,128)}, u32[]{:S(2)}, u32[]{:S(2)}) collective-permute-start(f32[1,135,128]{1,2,0:T(8,128)} %select_bitcast_fusion), channel_id=1, source_target_pairs={{1,0},{2,1},{3,2},{4,3},{5,4},{6,5},{7,6},{8,7},{9,8},{10,9},{11,1... | collective-permute-start | bytes 207368 | tf_op jit(solution)/shard_map/ppermute | solution.py:25
  74.1 18.2 %copy-start.31 = (f32[3,3,128]{1,0,2:T(4,128)}, f32[3,3,128]{1,0,2:T(4,128)S(1)}, u32[]{:S(2)}) copy-start(f32[3,3,128]{1,0,2:T(4,128)S(1)} %copy.422) | copy-start | bytes 13828
  117.5 19.0 %copy-start.136 = (s32[32]{0:T(128)S(1)}, s32[32]{0:T(128)}, u32[]{:S(2)}) copy-start(s32[32]{0:T(128)} %get-tuple-element.16) | copy-start | bytes 388
  121.5 18.7 %copy-start.51 = (pred[15,4,256]{0,2,1:T(8,128)(4,1)S(1)}, pred[15,4,256]{0,2,1:T(8,128)(4,1)}, u32[]{:S(2)}) copy-start(pred[15,4,256]{0,2,1:T(8,128)(4,1)} %compare_and_fusion) | copy-start | bytes 46084
  121.6 22.8 %copy-start.43 = (f32[135,256]{1,0:T(8,128)S(1)}, f32[135,256]{1,0:T(8,128)}, u32[]{:S(2)}) copy-start(f32[135,256]{1,0:T(8,128)} %copy-done.42) | copy-start | bytes 414724
  124.5 20.0 %copy-start.113 = (s32[1024]{0:T(1024)}, s32[1024]{0:T(1024)S(1)}, u32[]{:S(2)}) copy-start(s32[1024]{0:T(1024)S(1)} %pad_clamp_fusion.7) | copy-start | bytes 12292
  124.6 8.7 %all-to-all-start.1 = ((f32[135,4,8]{0,2,1:T(8,128)}), f32[135,4,8]{0,2,1:T(8,128)S(1)}, u32[]{:S(2)}, u32[]{:S(2)}) async-start(f32[135,4,8]{0,2,1:T(8,128)} %select_bitcast_fusion.13), calls=%async_computation.1 | async-start | bytes 65536 | tf_op jit(solution)/shard_map/all_to_all | solution.py:176
  127.9 16.7 %copy-start.114 = (s32[1024]{0:T(1024)}, s32[1024]{0:T(1024)S(1)}, u32[]{:S(2)}) copy-start(s32[1024]{0:T(1024)S(1)} %pad_clamp_fusion.3) | copy-start | bytes 12292
  133.3 8.7 %all-to-all-start.3 = ((f32[135,4,8]{0,2,1:T(8,128)}), f32[135,4,8]{0,2,1:T(8,128)S(1)}, u32[]{:S(2)}, u32[]{:S(2)}) async-start(f32[135,4,8]{0,2,1:T(8,128)} %select_bitcast_fusion.6), calls=%async_computation.3 | async-start | bytes 65536 | tf_op jit(solution)/shard_map/all_to_all | solution.py:177
  165.3 12.2 %collective-permute-start.3 = (f32[1,135,32]{1,2,0:T(8,128)}, f32[1,135,32]{1,2,0:T(8,128)}, u32[]{:S(2)}, u32[]{:S(2)}) collective-permute-start(f32[1,135,32]{1,2,0:T(8,128)} %select_bitcast_fusion.11), channel_id=1, source_target_pairs={{1,0},{2,1},{3,2},{4,3},{5,4},{6,5},{7,6},{8,7},{9,8},{10,9},{11,1... | collective-permute-start | bytes 51848 | tf_op jit(solution)/shard_map/ppermute | solution.py:25
  167.2 11.1 %collective-permute-start.2 = (f32[1,135,32]{1,2,0:T(8,128)}, f32[1,135,32]{1,2,0:T(8,128)}, u32[]{:S(2)}, u32[]{:S(2)}) collective-permute-start(f32[1,135,32]{1,2,0:T(8,128)} %select_bitcast_fusion.12), channel_id=1, source_target_pairs={{0,1},{1,2},{2,3},{3,4},{4,5},{5,6},{6,7},{7,8},{8,9},{9,10},{10,1... | collective-permute-start | bytes 51848 | tf_op jit(solution)/shard_map/ppermute | solution.py:22
  201.2 20.4 %collective-permute-start.5 = (f32[1,135,32]{1,2,0:T(8,128)}, f32[1,135,32]{1,2,0:T(8,128)}, u32[]{:S(2)}, u32[]{:S(2)}) collective-permute-start(f32[1,135,32]{1,2,0:T(8,128)} %select_bitcast_fusion.9), channel_id=1, source_target_pairs={{1,0},{2,1},{3,2},{4,3},{5,4},{6,5},{7,6},{8,7},{9,8},{10,9},{11,1... | collective-permute-start | bytes 51848 | tf_op jit(solution)/shard_map/ppermute | solution.py:25
  208.3 14.2 %collective-permute-start.4 = (f32[1,135,32]{1,2,0:T(8,128)}, f32[1,135,32]{1,2,0:T(8,128)}, u32[]{:S(2)}, u32[]{:S(2)}) collective-permute-start(f32[1,135,32]{1,2,0:T(8,128)} %select_bitcast_fusion.10), channel_id=1, source_target_pairs={{0,1},{1,2},{2,3},{3,4},{4,5},{5,6},{6,7},{7,8},{8,9},{9,10},{10,1... | collective-permute-start | bytes 51848 | tf_op jit(solution)/shard_map/ppermute | solution.py:22
  216.3 154.5 %collective-permute-start.12 = (f32[1,135,128]{1,2,0:T(8,128)}, f32[1,135,128]{1,2,0:T(8,128)}, u32[]{:S(2)}, u32[]{:S(2)}) collective-permute-start(f32[1,135,128]{1,2,0:T(8,128)} %select_bitcast_fusion.1), channel_id=1, source_target_pairs={{0,1},{1,2},{2,3},{3,4},{4,5},{5,6},{6,7},{7,8},{8,9},{9,10},{10,1... | collective-permute-start | bytes 207368 | tf_op jit(solution)/shard_map/ppermute | solution.py:22
  243.2 21.0 %copy-start.18 = (f32[3,3,64]{1,0,2:T(4,128)S(1)}, f32[3,3,64]{1,0,2:T(4,128)}, u32[]{:S(2)}) copy-start(f32[3,3,64]{1,0,2:T(4,128)} %copy-done.15) | copy-start | bytes 6916
  246.2 21.7 %all-to-all-start.2 = ((f32[135,4,8]{0,2,1:T(8,128)}), f32[135,4,8]{0,2,1:T(8,128)}, u32[]{:S(2)}, u32[]{:S(2)}) async-start(f32[135,4,8]{0,2,1:T(8,128)} %get-tuple-element.83), calls=%async_computation.2 | async-start | bytes 65536 | tf_op jit(solution)/shard_map/all_to_all | solution.py:198
  252.2 95.0 %collective-permute-start.7 = (f32[1,135,32]{1,2,0:T(8,128)}, f32[1,135,32]{1,2,0:T(8,128)}, u32[]{:S(2)}, u32[]{:S(2)}) collective-permute-start(f32[1,135,32]{1,2,0:T(8,128)} %select_bitcast_fusion.7), channel_id=1, source_target_pairs={{1,0},{2,1},{3,2},{4,3},{5,4},{6,5},{7,6},{8,7},{9,8},{10,9},{11,1... | collective-permute-start | bytes 51848 | tf_op jit(solution)/shard_map/ppermute | solution.py:25
  261.7 90.1 %collective-permute-start.6 = (f32[1,135,32]{1,2,0:T(8,128)}, f32[1,135,32]{1,2,0:T(8,128)}, u32[]{:S(2)}, u32[]{:S(2)}) collective-permute-start(f32[1,135,32]{1,2,0:T(8,128)} %select_bitcast_fusion.8), channel_id=1, source_target_pairs={{0,1},{1,2},{2,3},{3,4},{4,5},{5,6},{6,7},{7,8},{8,9},{9,10},{10,1... | collective-permute-start | bytes 51848 | tf_op jit(solution)/shard_map/ppermute | solution.py:22
  267.9 65.9 %all-to-all-start.4 = ((f32[135,4,8]{0,2,1:T(8,128)}), f32[135,4,8]{0,2,1:T(8,128)}, u32[]{:S(2)}, u32[]{:S(2)}) async-start(f32[135,4,8]{0,2,1:T(8,128)} %get-tuple-element.82), calls=%async_computation.4 | async-start | bytes 65536 | tf_op jit(solution)/shard_map/all_to_all | solution.py:199
  277.3 17.4 %copy-start.77 = (pred[7680]{0:T(1024)(128)(4,1)S(1)}, pred[7680]{0:T(1024)(128)(4,1)}, u32[]{:S(2)}) copy-start(pred[7680]{0:T(1024)(128)(4,1)} %compare_and_fusion.1) | copy-start | bytes 23044
  310.4 14.5 %copy-start.32 = (f32[3,3,128]{1,0,2:T(4,128)S(1)}, f32[3,3,128]{1,0,2:T(4,128)}, u32[]{:S(2)}) copy-start(f32[3,3,128]{1,0,2:T(4,128)} %copy-done.31) | copy-start | bytes 13828
  313.3 128.6 %collective-permute-start.11 = (f32[1,135,64]{1,2,0:T(8,128)}, f32[1,135,64]{1,2,0:T(8,128)}, u32[]{:S(2)}, u32[]{:S(2)}) collective-permute-start(f32[1,135,64]{1,2,0:T(8,128)} %select_bitcast_fusion.2), channel_id=1, source_target_pairs={{1,0},{2,1},{3,2},{4,3},{5,4},{6,5},{7,6},{8,7},{9,8},{10,9},{11,1... | collective-permute-start | bytes 103688 | tf_op jit(solution)/shard_map/ppermute | solution.py:25
  330.7 22.0 %copy-start.37 = (f32[135,32]{1,0:T(8,128)S(1)}, f32[135,32]{1,0:T(8,128)}, u32[]{:S(2)}) copy-start(f32[135,32]{1,0:T(8,128)} %copy-done.34) | copy-start | bytes 51844
  330.7 22.0 %copy-start.41 = (f32[135,32]{1,0:T(8,128)S(1)}, f32[135,32]{1,0:T(8,128)}, u32[]{:S(2)}) copy-start(f32[135,32]{1,0:T(8,128)} %copy-done.38) | copy-start | bytes 51844
  333.8 8.7 %all-to-all-start.5 = ((f32[135,4,8]{0,2,1:T(8,128)}), f32[135,4,8]{0,2,1:T(8,128)S(1)}, u32[]{:S(2)}, u32[]{:S(2)}) async-start(f32[135,4,8]{0,2,1:T(8,128)} %fusion.80), calls=%async_computation.5 | async-start | bytes 65536 | tf_op jit(solution)/shard_map/all_to_all | solution.py:200
  337.1 15.8 %copy-start.75 = (f32[9,35,128]{2,1,0:T(8,128)}, f32[9,35,128]{2,1,0:T(8,128)S(1)}, u32[]{:S(2)}) copy-start(f32[9,35,128]{2,1,0:T(8,128)S(1)} %constant_dynamic-update-slice_fusion.45) | copy-start | bytes 483844
  343.2 28.6 %all-to-all-start.6 = ((f32[135,4,8]{0,2,1:T(8,128)}), f32[135,4,8]{0,2,1:T(8,128)}, u32[]{:S(2)}, u32[]{:S(2)}) async-start(f32[135,4,8]{0,2,1:T(8,128)} %fusion.78), calls=%async_computation.6 | async-start | bytes 65536 | tf_op jit(solution)/shard_map/all_to_all | solution.py:215
  347.1 95.7 %collective-permute-start.10 = (f32[1,135,64]{1,2,0:T(8,128)}, f32[1,135,64]{1,2,0:T(8,128)}, u32[]{:S(2)}, u32[]{:S(2)}) collective-permute-start(f32[1,135,64]{1,2,0:T(8,128)} %select_bitcast_fusion.3), channel_id=1, source_target_pairs={{0,1},{1,2},{2,3},{3,4},{4,5},{5,6},{6,7},{7,8},{8,9},{9,10},{10,1... | collective-permute-start | bytes 103688 | tf_op jit(solution)/shard_map/ppermute | solution.py:22
  (118 other events, 559.8 us)
where the time goes:
time: 484 us; the launch traced here: 477 us
  local copies, waits for them, and re-layouts  254 us (52%)
  starting transfers between devices  98.3 us (20%)
  other arithmetic  60.7 us (13%)
  matrix products  51.2 us (11%)
  waiting for transfers between devices  9.32 us (2%)
    gather x8, local copies, waits for them, and re-layouts, element_rate(): jnp.take(flat_table, flat_index.reshape(-1), axis=1)  127 us
    ppermute x7, starting transfers between devices, padded(): lax.ppermute(lax.slice_in_dim(block, 0, width, axis=dim), axis, backward)  54.5 us
    dot_general x7, matrix products, element_rate(): jnp.einsum('ike,kqme->iqme', geometry, along_ref, precision=highest)  34.5 us
    select_n x9, other arithmetic, element_rate(): jnp.take(flat_table, flat_index.reshape(-1), axis=1)  28.4 us
    reshape x14, local copies, waits for them, and re-layouts, element_rate(): flat_table = trace_table.reshape(9, 15 * columns)  25.2 us
    ppermute x7, starting transfers between devices, padded(): lax.ppermute(lax.slice_in_dim(block, block.shape[dim] - width, None, axis...  17.7 us
    transpose x7, local copies, waits for them, and re-layouts, element_rate(): jnp.einsum('kmn,qne->kqme', derivative, element_state, precision=highest)  12 us
    dot_general x7, local copies, waits for them, and re-layouts, element_rate(): jnp.einsum('ike,kqme->iqme', geometry, along_ref, precision=highest)  11.2 us
  transfers between devices with their start and end apart: 21, of which 2 were waited for; matrix products, arithmetic and copies ran while one was open for 67% of the time, Pallas kernels for 0%

commit v1 on v0

v1 whole, which is shorter than its diff:
```python
import functools

import jax
import jax.numpy as jnp
import numpy as np
from jax import lax
from jax.experimental import pallas as pl
from jax.experimental.pallas import tpu as pltpu
from jax.sharding import PartitionSpec as P

F32 = jnp.float32
BF16 = jnp.bfloat16
MESH = pl.DeviceIdType.MESH
N_SUB = 4
COARSE_STEP = 0.1

LANE = (0, 64, 192)
WIDE = (128, 128, 256)
OWN = (512, 512, 1024)
EXT = (128, 256, 384)
SENT = (128, 256, 384)
STEP = (COARSE_STEP / 4, COARSE_STEP / 2, COARSE_STEP)

VOIGT = ((3, 8, 7), (8, 4, 6), (7, 6, 5))


def face_tables():
    lattice = [
        (a, b, c, 4 - a - b - c) for a in range(5) for b in range(5 - a) for c in range(5 - a - b)
    ]
    face_rows = np.array(
        [[i for i, p in enumerate(lattice) if p[f] == 0] for f in range(4)], np.int32
    )
    triangle = [p[1:] for p in lattice if p[0] == 0]
    position = {p: i for i, p in enumerate(triangle)}

    def turned(p, times):
        p = (p[1], p[0], p[2])
        for _ in range(times):
            p = (p[1], p[2], p[0])
        return p

    orders = np.array(
        [[position[turned(p, o)] for p in triangle] for o in range(3)], np.int32
    )
    return face_rows, orders


def constants():
    face_rows, orders = face_tables()
    place = np.zeros((2, 128, 144), np.float32)
    for n in range(35):
        place[0, n, n] = 1
        place[0, n, 48 + n] = 1
        place[1, n, 96 + n] = 1
    select = np.zeros((128, 144), np.float32)
    for f in range(4):
        for n in range(15):
            select[f * 16 + n, face_rows[f, n]] = 1
            select[64 + f * 16 + n, 48 + face_rows[f, n]] = 1
    spread = np.zeros((128, 256), np.float32)
    for f in range(4):
        for n in range(15):
            for o in range(3):
                spread[f * 15 + n, (o * 4 + f) * 16 + orders[o, n]] = 1
            spread[f * 15 + n, 192 + f * 16 + n] = -1
    return place, select, spread


def split(x):
    high = x.astype(BF16)
    return high, (x - high.astype(F32)).astype(BF16)


def dot(a, b):
    return jnp.dot(a, b, preferred_element_type=F32)


def lanes(shape):
    return lax.broadcasted_iota(jnp.int32, shape, 1)


def turn(x, shift):
    shift %= 128
    return pltpu.roll(x, shift, 1) if shift else x


def one_hot(rows, base, index):
    iota = lax.broadcasted_iota(jnp.int32, (rows, index.shape[1]), 0)
    hit = iota == jnp.broadcast_to(index - base, iota.shape)
    return jnp.where(hit, 1.0, 0.0).astype(BF16)


def kernel(
    n_dom,
    wave, mat, geo, fs, der, lift, nbr, ori, halo, iface, place, select, spread,
    out,
    u0, u1, u2, v0, v1, v2, t0, t1, t2, g0, g1, g2, stack, prod, jump,
    oh0, oh1, oh2, os0, os1, os2, cf0, cf1, cf2, sc0, sc1, sc2, om0, om1, om2,
    dpad, lpad, amat, lmat, sent0, sent1, sent2, sum_a, sum_b, base0,
    hs0, hr0, hs1, hr1, hs2, hr2, gs0, gr0, gs1, gr1, gs2, gr2, gs3, gr3,
    ss0, rs0, ss1, rs1, ss2, rs2, gss, grs,
):
    us, vs, ts, gs_, ohs, oss = (u0, u1, u2), (v0, v1, v2), (t0, t1, t2), (g0, g1, g2), (oh0, oh1, oh2), (os0, os1, os2)
    cfs, scs, oms, sents = (cf0, cf1, cf2), (sc0, sc1, sc2), (om0, om1, om2), (sent0, sent1, sent2)
    total = n_dom * N_SUB
    dom = lax.axis_index("dom")
    sub = lax.axis_index("sub")
    me = dom * N_SUB + sub
    up = (me + 1) % total
    down = (me + total - 1) % total
    up_id = (up // N_SUB, up % N_SUB)
    down_id = (down // N_SUB, down % N_SUB)
    not_first = jnp.where(me == 0, 0.0, 1.0).astype(F32)
    not_last = jnp.where(me == total - 1, 0.0, 1.0).astype(F32)

    barrier = pltpu.get_barrier_semaphore()
    pl.semaphore_signal(barrier, inc=1, device_id=up_id, device_id_type=MESH)
    pl.semaphore_signal(barrier, inc=1, device_id=down_id, device_id_type=MESH)
    for k in range(1, N_SUB):
        pl.semaphore_signal(
            barrier, inc=1, device_id=(dom, (sub + k) % N_SUB), device_id_type=MESH
        )

    def halo_copies(send, recv, ssem, rsem, slot):
        return [
            pltpu.make_async_remote_copy(
                src_ref=send.at[slot, way], dst_ref=recv.at[slot, way],
                send_sem=ssem.at[slot, way], recv_sem=rsem.at[slot, way],
                device_id=(up_id, down_id)[way], device_id_type=MESH,
            )
            for way in range(2)
        ]

    def group_copies(send, recv, number):
        found = []
        for k in range(1, N_SUB):
            dest = (sub + k) % N_SUB
            found.append(
                pltpu.make_async_remote_copy(
                    src_ref=send.at[dest], dst_ref=recv.at[sub],
                    send_sem=gss.at[number, k], recv_sem=grs.at[number, k],
                    device_id=(dom, dest), device_id_type=MESH,
                )
            )
        return found

    halo_f = [halo_copies(hs0, hr0, ss0, rs0, s) for s in range(4)]
    halo_m = [halo_copies(hs1, hr1, ss1, rs1, s) for s in range(2)]
    halo_c = halo_copies(hs2, hr2, ss2, rs2, 0)
    group = [
        group_copies(s, r, i)
        for i, (s, r) in enumerate(((gs0, gr0), (gs1, gr1), (gs2, gr2), (gs3, gr3)))
    ]

    dpad[...] = jnp.zeros_like(dpad)
    lpad[...] = jnp.zeros_like(lpad)
    for k in range(3):
        dpad[k, 0:35, 0:35] = der[k]
    lpad[0:35, 0:60] = lift[...]
    parts = []
    for k in range(3):
        high, low = split(dpad[k])
        parts.append(dot(high, place[0]) + dot(low, place[1]))
    amat[...] = jnp.concatenate(parts + [select[...]], axis=0).astype(BF16)
    high, low = split(lpad[...])
    lmat[0:48] = dot(high, spread[...]).astype(BF16)
    lmat[48:96] = dot(low, spread[...]).astype(BF16)

    def remap(index, c):
        if c:
            return index
        return jnp.where(
            index < 256, (index & 63) + ((index >> 6) << 7), index + 256
        )

    def load(c):
        first, wide = LANE[c], WIDE[c]
        span = slice(first, first + wide)
        u = us[c]
        for q in range(9):
            u[q, 32:40, :] = jnp.zeros((8, wide), F32)
            u[q, 0:35, :] = wave[q, :, span]
        rho = STEP[c] / mat[0:1, span]
        lam = STEP[c] * mat[1:2, span]
        mu = STEP[c] * mat[2:3, span]
        cf = cfs[c]
        for i in range(3):
            axes = geo[i, :, span]
            cf[3 * i : 3 * i + 3] = axes * mu
            cf[9 + 3 * i : 12 + 3 * i] = axes * rho
            cf[18 + 3 * i : 21 + 3 * i] = axes
        cf[27:28] = lam
        cf[28:29] = 2.0 * mu
        for f in range(4):
            where = slice(f * wide, (f + 1) * wide)
            scs[c][:, where] = (0.5 * STEP[c]) * fs[f : f + 1, span]
            row = jnp.broadcast_to(ori[f : f + 1, span], (16, wide))
            for o in range(3):
                oms[c][o, :, where] = jnp.where(row == o, 1.0, 0.0).astype(BF16)

    def send_tables():
        low, high = halo[0:1, 0:32], halo[1:2, 0:32]
        row = jnp.concatenate([low, high, iface[0, 0:1], iface[0, 1:2]], axis=1)
        os0[...] = one_hot(512, 0, remap(row, 0))
        row = jnp.concatenate([halo[0:1, 32:96], halo[1:2, 32:96]], axis=1)
        os1[:, 0:128] = one_hot(512, 0, row)
        blank = jnp.full((1, 64), -1, jnp.int32)
        row = jnp.concatenate([iface[1, 0:1], iface[0, 2:3], blank], axis=1)
        os1[:, 128:256] = one_hot(512, 0, row)
        os2[:, 0:128] = one_hot(1024, 0, halo[0:1, 96:224])
        os2[:, 128:256] = one_hot(1024, 0, halo[1:2, 96:224])
        row = jnp.concatenate([iface[1, 1:2], iface[1, 2:3], blank], axis=1)
        os2[:, 256:384] = one_hot(1024, 0, row)

    def neighbour_table(c):
        span = slice(LANE[c], LANE[c] + WIDE[c])
        for f in range(4):
            where = slice(f * WIDE[c], (f + 1) * WIDE[c])
            index = remap(nbr[f : f + 1, span], c)
            ohs[c][:, where] = one_hot(OWN[c] + EXT[c], 0, index)

    def traces(c):
        wide = WIDE[c]
        u, t = us[c], ts[c]
        gap = jnp.zeros((8, wide), F32)
        for q in range(9):
            x = u[q]
            high = x.astype(BF16).astype(F32)
            tall = jnp.concatenate([high, gap, x - high, gap, high, gap], axis=0)
            stack[:, q * wide : (q + 1) * wide] = tall.astype(BF16)
        span = 9 * wide
        prod[:, 0:span] = dot(amat[...], stack[:, 0:span])
        for q in range(9):
            where = slice(q * wide, (q + 1) * wide)
            for part in range(2):
                for f in range(4):
                    row = 120 + 64 * part + 16 * f
                    t[144 * part + 16 * q : 144 * part + 16 * q + 16, f * wide : (f + 1) * wide] = (
                        prod[row : row + 16, where].astype(BF16)
                    )
        both = dot(t[:, 0 : OWN[c]], oss[c][...])
        sents[c][...] = both[0:144] + both[144:288]

    def volume(c):
        wide = WIDE[c]
        cf = cfs[c]
        for start in range(0, wide, 128):
            span = slice(start, start + 128)

            def grad(q, i, kind):
                at = q * wide + start
                base = 9 * kind + 3 * i
                return sum(
                    jnp.broadcast_to(cf[base + k : base + k + 1, span], (40, 128))
                    * prod[40 * k : 40 * k + 40, at : at + 128]
                    for k in range(3)
                )

            for i in range(3):
                rate = grad(VOIGT[i][0], 0, 1) + grad(VOIGT[i][1], 1, 1) + grad(VOIGT[i][2], 2, 1)
                vs[c][i, :, span] = us[c][i, :, span] + rate
            diag = [grad(i, i, 2) for i in range(3)]
            shared = cf[27:28, span] * (diag[0] + diag[1] + diag[2])
            for i in range(3):
                vs[c][3 + i, :, span] = us[c][3 + i, :, span] + (shared + cf[28:29, span] * diag[i])
            for q, i, j in ((6, 1, 2), (7, 0, 2), (8, 0, 1)):
                rate = grad(j, i, 0) + grad(i, j, 0)
                vs[c][q, :, span] = us[c][q, :, span] + rate
        both = dot(ts[c][:, 0 : OWN[c]], ohs[c][0 : OWN[c]])
        gs_[c][...] = both[0:144] + both[144:288]

    def store_ext(c, at, value):
        high, low = split(value)
        ts[c][0:144, OWN[c] + at : OWN[c] + at + 128] = high
        ts[c][144:288, OWN[c] + at : OWN[c] + at + 128] = low

    def finish(c):
        wide, own = WIDE[c], OWN[c]
        t = ts[c]
        both = dot(t[:, own:], ohs[c][own:])
        gs_[c][...] += both[0:144] + both[144:288]
        scale = scs[c][...]
        for q in range(9):
            rows = slice(16 * q, 16 * q + 16)
            low_rows = slice(144 + 16 * q, 160 + 16 * q)
            high, low = split(gs_[c][rows] * scale)
            mine = t[rows, 0:own].astype(F32) + t[low_rows, 0:own].astype(F32)
            own_high, own_low = split(mine * scale)
            where = slice(q * wide, (q + 1) * wide)
            for f in range(4):
                face = slice(f * wide, (f + 1) * wide)
                for o in range(3):
                    mask = oms[c][o, :, face]
                    at = (4 * o + f) * 16
                    jump[0, at : at + 16, where] = high[:, face] * mask
                    jump[1, at : at + 16, where] = low[:, face] * mask
                at = 192 + 16 * f
                jump[0, at : at + 16, where] = own_high[:, face]
                jump[1, at : at + 16, where] = own_low[:, face]
        span = 9 * wide
        first = dot(lmat[...], jump[0, :, 0:span])
        second = dot(lmat[0:48], jump[1, :, 0:span])
        whole = first[0:40] + first[48:88] + second[0:40]
        for q in range(9):
            us[c][q] = vs[c][q] + whole[:, q * wide : (q + 1) * wide]

    lane48 = lanes((48, 128))
    lane16 = lanes((16, 128))

    def pack_third(x, base):
        return jnp.where(
            lane48 < 32, turn(x[0:48], -base),
            jnp.where(lane48 < 64, turn(x[48:96], 32 - base), turn(x[96:144], 64 - base)),
        )

    def send_fine(slot):
        x = sent0[...]
        hs0[slot, 0] = pack_third(x, 32)
        hs0[slot, 1] = pack_third(x, 0)

    def send_middle(slot):
        x = sent1[:, 0:128]
        lower = x[0:80]
        upper = jnp.concatenate([x[80:144], jnp.zeros((16, 128), F32)], axis=0)
        left = lanes((80, 128)) < 64
        hs1[slot, 0] = jnp.where(left, turn(lower, 64), upper)
        hs1[slot, 1] = jnp.where(left, lower, turn(upper, 64))

    def send_group(send, recv, number, x, base):
        rows = slice(16 * number, 16 * number + 16)
        for j in range(N_SUB):
            acc = jnp.zeros((16, 128), F32)
            for q in range(9):
                piece = turn(x[16 * q : 16 * q + 16], 8 * q - base - 8 * j)
                acc = jnp.where((lane16 >= 8 * q) & (lane16 < 8 * q + 8), piece, acc)
            send[j, rows] = acc
        recv[sub, rows] = send[sub, rows]

    def take_group(recv, number, base):
        rows = slice(16 * number, 16 * number + 16)
        pieces = [recv[p, rows] for p in range(N_SUB)]
        found = []
        for q in range(9):
            acc = jnp.zeros((16, 128), F32)
            for p in range(N_SUB):
                at = base + 8 * p
                acc = jnp.where(
                    (lane16 >= at) & (lane16 < at + 8), turn(pieces[p], at - 8 * q), acc
                )
            found.append(acc)
        return jnp.concatenate(found, axis=0)

    def start(copies):
        for copy in copies:
            copy.start()

    def arrive(copies):
        for copy in copies:
            copy.wait_recv()

    def fine_ext(slot):
        below = hr0[slot, 0] * not_first
        above = hr0[slot, 1] * not_last
        found = []
        for r in range(3):
            found.append(
                jnp.where(
                    lane48 < 32, turn(below, -32 * r),
                    jnp.where(lane48 < 64, turn(above, 32 - 32 * r), base0[48 * r : 48 * r + 48]),
                )
            )
        store_ext(0, 0, jnp.concatenate(found, axis=0))

    def middle_ext(slot):
        below = hr1[slot, 0] * not_first
        above = hr1[slot, 1] * not_last
        left = lanes((80, 128)) < 64
        lower = jnp.where(left, below, turn(above, 64))
        upper = jnp.where(left, turn(below, 64), above)
        store_ext(1, 0, jnp.concatenate([lower, upper[0:64]], axis=0))

    load(0)
    send_tables()
    traces(0)
    sum_a[...] = sent0[...]
    send_fine(0)
    pl.semaphore_wait(barrier, 2 + N_SUB - 1)
    start(halo_f[0])
    neighbour_table(0)
    volume(0)
    load(1)
    traces(1)
    send_middle(0)
    start(halo_m[0])
    sum_b[...] = sent1[:, 128:256]
    send_group(gs0, gr0, 0, sent1[:, 128:256], 0)
    neighbour_table(1)
    volume(1)
    load(2)
    traces(2)
    send_group(gs0, gr0, 1, sent2[:, 256:384], 0)
    send_group(gs0, gr0, 2, sent2[:, 256:384], 32)
    start(group[0])
    hs2[0, 0] = sent2[:, 128:256]
    hs2[0, 1] = sent2[:, 0:128]
    start(halo_c)
    neighbour_table(2)
    volume(2)
    arrive(group[0])
    base0[...] = take_group(gr0, 0, 64) + take_group(gr0, 1, 96)
    start_mc = take_group(gr0, 2, 32)

    arrive(halo_f[0])
    fine_ext(0)
    finish(0)
    traces(0)
    send_fine(1)
    start(halo_f[1])
    sum_a[...] += sent0[...]
    send_group(gs1, gr1, 0, 0.5 * sum_a[...], 64)
    start(group[1])
    volume(0)
    arrive(halo_m[0])
    middle_ext(0)

    arrive(halo_f[1])
    fine_ext(1)
    finish(0)
    traces(0)
    send_fine(2)
    start(halo_f[2])
    sum_a[...] = 0.25 * sum_a[...] + 0.25 * sent0[...]
    base1 = sent0[...]
    volume(0)

    arrive(group[1])
    store_ext(1, 128, take_group(gr1, 0, 0) + start_mc)
    finish(1)
    traces(1)
    send_middle(1)
    start(halo_m[1])
    send_group(gs2, gr2, 0, 0.5 * (sum_b[...] + sent1[:, 128:256]), 32)
    start(group[2])
    volume(1)

    arrive(halo_f[2])
    fine_ext(2)
    finish(0)
    traces(0)
    send_fine(3)
    start(halo_f[3])
    sum_a[...] += 0.25 * sent0[...]
    send_group(gs3, gr3, 0, 0.5 * (base1 + sent0[...]), 64)
    send_group(gs3, gr3, 1, sum_a[...], 96)
    start(group[3])
    volume(0)
    arrive(halo_c)
    store_ext(2, 0, hr2[0, 0] * not_first)
    store_ext(2, 128, hr2[0, 1] * not_last)
    arrive(halo_m[1])
    middle_ext(1)

    arrive(halo_f[3])
    fine_ext(3)
    finish(0)
    arrive(group[3])
    store_ext(1, 128, take_group(gr3, 0, 0) + start_mc)
    finish(1)
    arrive(group[2])
    store_ext(2, 256, take_group(gr3, 1, 0) + take_group(gr2, 0, 32))
    finish(2)
    for q in range(9):
        out[q, :, 0:64] = u0[q, 0:35, 0:64]
        out[q, :, 64:192] = u1[q, 0:35, :]
        out[q, :, 192:448] = u2[q, 0:35, :]
    for copies in halo_f + halo_m + [halo_c] + group:
        for copy in copies:
            copy.wait_send()


def scratch():
    shapes = []
    shapes += [pltpu.VMEM((9, 40, w), F32) for w in WIDE] * 2
    shapes += [pltpu.VMEM((288, o + e), BF16) for o, e in zip(OWN, EXT)]
    shapes += [pltpu.VMEM((144, o), F32) for o in OWN]
    shapes += [pltpu.VMEM((144, 9 * 256), BF16), pltpu.VMEM((248, 9 * 256), F32)]
    shapes += [pltpu.VMEM((2, 256, 9 * 256), BF16)]
    shapes += [pltpu.VMEM((o + e, o), BF16) for o, e in zip(OWN, EXT)]
    shapes += [pltpu.VMEM((o, s), BF16) for o, s in zip(OWN, SENT)]
    shapes += [pltpu.VMEM((32, w), F32) for w in WIDE]
    shapes += [pltpu.VMEM((1, o), F32) for o in OWN]
    shapes += [pltpu.VMEM((3, 16, o), BF16) for o in OWN]
    shapes += [pltpu.VMEM((3, 40, 128), F32), pltpu.VMEM((48, 128), F32)]
    shapes += [pltpu.VMEM((248, 144), BF16), pltpu.VMEM((96, 256), BF16)]
    shapes += [pltpu.VMEM((144, s), F32) for s in SENT]
    shapes += [pltpu.VMEM((144, 128), F32)] * 3
    shapes += [pltpu.VMEM((4, 2, 48, 128), F32)] * 2
    shapes += [pltpu.VMEM((2, 2, 80, 128), F32)] * 2
    shapes += [pltpu.VMEM((1, 2, 144, 128), F32)] * 2
    for buffers in (3, 1, 1, 2):
        shapes += [pltpu.VMEM((N_SUB, 16 * buffers, 128), F32)] * 2
    for slots in (4, 2, 1):
        shapes += [pltpu.SemaphoreType.DMA((slots, 2))] * 2
    shapes += [pltpu.SemaphoreType.DMA((4, 4))] * 2
    return shapes


def solution(mesh):
    n_dom = mesh.shape["dom"]
    place, select, spread = constants()

    def on_device(*arrays):
        consts = (
            jnp.asarray(place, BF16), jnp.asarray(select, F32), jnp.asarray(spread, BF16),
        )
        return pl.pallas_call(
            functools.partial(kernel, n_dom),
            out_shape=jax.ShapeDtypeStruct(arrays[0].shape, F32),
            in_specs=[pl.BlockSpec(memory_space=pltpu.VMEM)] * 13,
            out_specs=pl.BlockSpec(memory_space=pltpu.VMEM),
            scratch_shapes=scratch(),
            compiler_params=pltpu.CompilerParams(
                collective_id=0, has_side_effects=True, vmem_limit_bytes=60 * 1024 * 1024
            ),
            name="step",
        )(*arrays, *consts)

    split_all = ("dom", "sub")
    placed = (
        P(None, None, split_all), P(None, split_all), P(None, None, split_all),
        P(None, split_all), P(), P(), P(None, split_all), P(None, split_all),
        P(None, split_all), P(None, None, split_all),
    )
    return jax.shard_map(
        on_device, mesh=mesh, in_specs=placed, out_specs=P(None, None, split_all), check_vma=False,
    )
```

time: 484 us -> 48.8 us (0.10)
  the two profiles are of different devices: /device:TPU:512 before, /device:TPU:2 now
where the time goes in v1:
time: 48.8 us; the launch traced here: 48.6 us
  Pallas kernels  45.2 us (93%)
  local copies, waits for them, and re-layouts  3.3 us (7%)
    pallas_call x1, Pallas kernels, on_device(): pl.pallas_call(functools.partial(kernel, n_dom), out_shape=jax.ShapeDtype...  45.2 us
    unnamed x2, local copies, waits for them, and re-layouts  3.3 us

profile of v1, /device:TPU:2, one launch (start us, length us, event | category | flops | bytes accessed | tf_op | source)
XLA Modules:
  0.0 48.6 jit_solution(11641280008240998857)
XLA Ops:
  0.0 1.3 %copy.14.iface = s32[2,3,32]{2,1,0:T(4,128)} copy(s32[2,3,32]{2,0,1:T(2,128)} %param.22) | data formatting | bytes 1536 | tf_op args[9]
  1.3 45.2 %step.1 = f32[9,35,448]{2,1,0:T(8,128)} custom-call(f32[9,35,448]{2,1,0:T(8,128)} %wave.1, f32[3,448]{1,0:T(4,128)} %mat.1, f32[3,3,448]{2,1,0:T(4,128)} %geo.1, f32[4,448]{1,0:T(4,128)} %fs.1, f32[3,35,35]{2,1,0:T(8,128)} %der.1, f32[35,60]{1,0:T(8,128)} %lift.1, s32[4,448]{1,0:T(4,128)} %nbr.1, s32[4,448]{1,0:T(4,128)} %ori.1, s32[2,224]{1,0:T(2,128)} %halo.1, ...), custom_call_target="tpu_custom_call" | custom-call | tf_op jit(solution)/shard_map/step/pallas_call | solution.py:517
  46.5 2.0 %copy.16 = f32[9,35,448]{2,1,0:T(8,128)} copy(f32[9,35,448]{2,1,0:T(8,128)} %step.1) | data formatting | bytes 1128960

commit v2 on v1

--- a/solution.py
+++ b/solution.py
@@ -93,9 +93,16 @@
 
 def kernel(
     n_dom,
+    *refs,
+):
+    ins, out, held, in_sems, rest = refs[:13], refs[13], refs[14:27], refs[27], refs[28:]
+    body(n_dom, ins, in_sems, out, *held, *rest)
+
+
+def body(
+    n_dom, ins, in_sems, out,
     wave, mat, geo, fs, der, lift, nbr, ori, halo, iface, place, select, spread,
-    out,
-    u0, u1, u2, v0, v1, v2, t0, t1, t2, g0, g1, g2, stack, prod, jump,
+    u0, u1, u2, v0, v1, v2, t0, t1, t2, g0, g1, g2, stack, prod0, prod1, prod2, jump,
     oh0, oh1, oh2, os0, os1, os2, cf0, cf1, cf2, sc0, sc1, sc2, om0, om1, om2,
     dpad, lpad, amat, lmat, sent0, sent1, sent2, sum_a, sum_b, base0,
     hs0, hr0, hs1, hr1, hs2, hr2, gs0, gr0, gs1, gr1, gs2, gr2, gs3, gr3,
@@ -103,6 +110,7 @@
 ):
     us, vs, ts, gs_, ohs, oss = (u0, u1, u2), (v0, v1, v2), (t0, t1, t2), (g0, g1, g2), (oh0, oh1, oh2), (os0, os1, os2)
     cfs, scs, oms, sents = (cf0, cf1, cf2), (sc0, sc1, sc2), (om0, om1, om2), (sent0, sent1, sent2)
+    prods = (prod0, prod1, prod2)
     total = n_dom * N_SUB
     dom = lax.axis_index("dom")
     sub = lax.axis_index("sub")
@@ -111,12 +119,18 @@
     down = (me + total - 1) % total
     up_id = (up // N_SUB, up % N_SUB)
     down_id = (down // N_SUB, down % N_SUB)
-    not_first = jnp.where(me == 0, 0.0, 1.0).astype(F32)
-    not_last = jnp.where(me == total - 1, 0.0, 1.0).astype(F32)
+    first, last = me == 0, me == total - 1
 
     barrier = pltpu.get_barrier_semaphore()
-    pl.semaphore_signal(barrier, inc=1, device_id=up_id, device_id_type=MESH)
-    pl.semaphore_signal(barrier, inc=1, device_id=down_id, device_id_type=MESH)
+
+    @pl.when(jnp.logical_not(last))
+    def _():
+        pl.semaphore_signal(barrier, inc=1, device_id=up_id, device_id_type=MESH)
+
+    @pl.when(jnp.logical_not(first))
+    def _():
+        pl.semaphore_signal(barrier, inc=1, device_id=down_id, device_id_type=MESH)
+
     for k in range(1, N_SUB):
         pl.semaphore_signal(
             barrier, inc=1, device_id=(dom, (sub + k) % N_SUB), device_id_type=MESH
@@ -145,6 +159,25 @@
             )
         return found
 
+    held = (wave, mat, geo, fs, der, lift, nbr, ori, halo, iface, place, select, spread)
+    fetch = {
+        i: pltpu.make_async_copy(ins[i], held[i], in_sems.at[i])
+        for i in (4, 5, 10, 11, 12, 0, 8, 9, 1, 2, 3, 7, 6)
+    }
+    for copy in fetch.values():
+        copy.start()
+
+    def fetched(*numbers):
+        for i in numbers:
+            fetch[i].wait()
+
+    for end, way in ((first, 0), (last, 1)):
+
+        @pl.when(end)
+        def _():
+            for ref in (hr0, hr1, hr2):
+                ref[:, way] = jnp.zeros((ref.shape[0],) + ref.shape[2:], F32)
+
     halo_f = [halo_copies(hs0, hr0, ss0, rs0, s) for s in range(4)]
     halo_m = [halo_copies(hs1, hr1, ss1, rs1, s) for s in range(2)]
     halo_c = halo_copies(hs2, hr2, ss2, rs2, 0)
@@ -155,6 +188,7 @@
 
     dpad[...] = jnp.zeros_like(dpad)
     lpad[...] = jnp.zeros_like(lpad)
+    fetched(4, 5, 10, 11, 12)
     for k in range(3):
         dpad[k, 0:35, 0:35] = der[k]
     lpad[0:35, 0:60] = lift[...]
@@ -181,6 +215,10 @@
         for q in range(9):
             u[q, 32:40, :] = jnp.zeros((8, wide), F32)
             u[q, 0:35, :] = wave[q, :, span]
+
+    def coefficients(c):
+        first, wide = LANE[c], WIDE[c]
+        span = slice(first, first + wide)
         rho = STEP[c] / mat[0:1, span]
         lam = STEP[c] * mat[1:2, span]
         mu = STEP[c] * mat[2:3, span]
@@ -199,19 +237,19 @@
             for o in range(3):
                 oms[c][o, :, where] = jnp.where(row == o, 1.0, 0.0).astype(BF16)
 
-    def send_tables():
-        low, high = halo[0:1, 0:32], halo[1:2, 0:32]
-        row = jnp.concatenate([low, high, iface[0, 0:1], iface[0, 1:2]], axis=1)
-        os0[...] = one_hot(512, 0, remap(row, 0))
-        row = jnp.concatenate([halo[0:1, 32:96], halo[1:2, 32:96]], axis=1)
-        os1[:, 0:128] = one_hot(512, 0, row)
+    def send_table(c):
         blank = jnp.full((1, 64), -1, jnp.int32)
-        row = jnp.concatenate([iface[1, 0:1], iface[0, 2:3], blank], axis=1)
-        os1[:, 128:256] = one_hot(512, 0, row)
-        os2[:, 0:128] = one_hot(1024, 0, halo[0:1, 96:224])
-        os2[:, 128:256] = one_hot(1024, 0, halo[1:2, 96:224])
-        row = jnp.concatenate([iface[1, 1:2], iface[1, 2:3], blank], axis=1)
-        os2[:, 256:384] = one_hot(1024, 0, row)
+        if c == 0:
+            rows = [(halo[0:1, 0:32], halo[1:2, 0:32], iface[0, 0:1], iface[1, 0:1])]
+        elif c == 1:
+            rows = [(halo[0:1, 32:96], halo[1:2, 32:96]), (iface[0, 1:2], iface[2, 0:1], blank)]
+        else:
+            rows = [
+                (halo[0:1, 96:224],), (halo[1:2, 96:224],), (iface[1, 1:2], iface[2, 1:2], blank),
+            ]
+        for i, row in enumerate(rows):
+            index = remap(jnp.concatenate(row, axis=1), c)
+            oss[c][:, 128 * i : 128 * i + 128] = one_hot(OWN[c], 0, index)
 
     def neighbour_table(c):
         span = slice(LANE[c], LANE[c] + WIDE[c])
@@ -222,7 +260,7 @@
 
     def traces(c):
         wide = WIDE[c]
-        u, t = us[c], ts[c]
+        u, t, prod = us[c], ts[c], prods[c]
         gap = jnp.zeros((8, wide), F32)
         for q in range(9):
             x = u[q]
@@ -230,7 +268,7 @@
             tall = jnp.concatenate([high, gap, x - high, gap, high, gap], axis=0)
             stack[:, q * wide : (q + 1) * wide] = tall.astype(BF16)
         span = 9 * wide
-        prod[:, 0:span] = dot(amat[...], stack[:, 0:span])
+        prod[...] = dot(amat[...], stack[:, 0:span])
         for q in range(9):
             where = slice(q * wide, (q + 1) * wide)
             for part in range(2):
@@ -244,7 +282,7 @@
 
     def volume(c):
         wide = WIDE[c]
-        cf = cfs[c]
+        cf, prod = cfs[c], prods[c]
         for start in range(0, wide, 128):
             span = slice(start, start + 128)
 
@@ -359,9 +397,17 @@
         for copy in copies:
             copy.wait_recv()
 
+    def start_halo(copies):
+        pl.when(jnp.logical_not(last))(copies[0].start)
+        pl.when(jnp.logical_not(first))(copies[1].start)
+
+    def arrive_halo(copies):
+        pl.when(jnp.logical_not(first))(copies[0].wait_recv)
+        pl.when(jnp.logical_not(last))(copies[1].wait_recv)
+
     def fine_ext(slot):
-        below = hr0[slot, 0] * not_first
-        above = hr0[slot, 1] * not_last
+        below = hr0[slot, 0]
+        above = hr0[slot, 1]
         found = []
         for r in range(3):
             found.append(
@@ -373,63 +419,69 @@
         store_ext(0, 0, jnp.concatenate(found, axis=0))
 
     def middle_ext(slot):
-        below = hr1[slot, 0] * not_first
-        above = hr1[slot, 1] * not_last
+        below = hr1[slot, 0]
+        above = hr1[slot, 1]
         left = lanes((80, 128)) < 64
         lower = jnp.where(left, below, turn(above, 64))
         upper = jnp.where(left, turn(below, 64), above)
         store_ext(1, 0, jnp.concatenate([lower, upper[0:64]], axis=0))
 
+    fetched(0, 8, 9)
     load(0)
-    send_tables()
+    send_table(0)
     traces(0)
     sum_a[...] = sent0[...]
     send_fine(0)
-    pl.semaphore_wait(barrier, 2 + N_SUB - 1)
-    start(halo_f[0])
-    neighbour_table(0)
-    volume(0)
+    pl.semaphore_wait(barrier, N_SUB - 1 + (me + total - 1) // total + 1 - (me + 1) // total)
+    start_halo(halo_f[0])
     load(1)
+    send_table(1)
     traces(1)
     send_middle(0)
-    start(halo_m[0])
     sum_b[...] = sent1[:, 128:256]
     send_group(gs0, gr0, 0, sent1[:, 128:256], 0)
-    neighbour_table(1)
-    volume(1)
     load(2)
+    send_table(2)
     traces(2)
     send_group(gs0, gr0, 1, sent2[:, 256:384], 0)
     send_group(gs0, gr0, 2, sent2[:, 256:384], 32)
-    start(group[0])
     hs2[0, 0] = sent2[:, 128:256]
     hs2[0, 1] = sent2[:, 0:128]
-    start(halo_c)
-    neighbour_table(2)
-    volume(2)
+    start(group[0])
+    start_halo(halo_m[0])
+    start_halo(halo_c)
+    fetched(1, 2, 3, 7, 6)
+    coefficients(0)
+    coefficients(1)
+    coefficients(2)
+    neighbour_table(0)
+    volume(0)
+    neighbour_table(1)
+    volume(1)
     arrive(group[0])
     base0[...] = take_group(gr0, 0, 64) + take_group(gr0, 1, 96)
     start_mc = take_group(gr0, 2, 32)
 
-    arrive(halo_f[0])
+    arrive_halo(halo_f[0])
     fine_ext(0)
     finish(0)
     traces(0)
     send_fine(1)
-    start(halo_f[1])
+    start_halo(halo_f[1])
     sum_a[...] += sent0[...]
     send_group(gs1, gr1, 0, 0.5 * sum_a[...], 64)
     start(group[1])
     volume(0)
-    arrive(halo_m[0])
+    neighbour_table(2)
+    arrive_halo(halo_m[0])
     middle_ext(0)
 
-    arrive(halo_f[1])
+    arrive_halo(halo_f[1])
     fine_ext(1)
     finish(0)
     traces(0)
     send_fine(2)
-    start(halo_f[2])
+    start_halo(halo_f[2])
     sum_a[...] = 0.25 * sum_a[...] + 0.25 * sent0[...]
     base1 = sent0[...]
     volume(0)
@@ -439,29 +491,30 @@
     finish(1)
     traces(1)
     send_middle(1)
-    start(halo_m[1])
+    start_halo(halo_m[1])
     send_group(gs2, gr2, 0, 0.5 * (sum_b[...] + sent1[:, 128:256]), 32)
     start(group[2])
     volume(1)
 
-    arrive(halo_f[2])
+    arrive_halo(halo_f[2])
     fine_ext(2)
     finish(0)
     traces(0)
     send_fine(3)
-    start(halo_f[3])
+    start_halo(halo_f[3])
     sum_a[...] += 0.25 * sent0[...]
     send_group(gs3, gr3, 0, 0.5 * (base1 + sent0[...]), 64)
     send_group(gs3, gr3, 1, sum_a[...], 96)
     start(group[3])
     volume(0)
-    arrive(halo_c)
-    store_ext(2, 0, hr2[0, 0] * not_first)
-    store_ext(2, 128, hr2[0, 1] * not_last)
-    arrive(halo_m[1])
+    volume(2)
+    arrive_halo(halo_c)
+    store_ext(2, 0, hr2[0, 0])
+    store_ext(2, 128, hr2[0, 1])
+    arrive_halo(halo_m[1])
     middle_ext(1)
 
-    arrive(halo_f[3])
+    arrive_halo(halo_f[3])
     fine_ext(3)
     finish(0)
     arrive(group[3])
@@ -474,17 +527,21 @@
         out[q, :, 0:64] = u0[q, 0:35, 0:64]
         out[q, :, 64:192] = u1[q, 0:35, :]
         out[q, :, 192:448] = u2[q, 0:35, :]
-    for copies in halo_f + halo_m + [halo_c] + group:
+    for copies in halo_f + halo_m + [halo_c]:
+        pl.when(jnp.logical_not(last))(copies[0].wait_send)
+        pl.when(jnp.logical_not(first))(copies[1].wait_send)
+    for copies in group:
         for copy in copies:
             copy.wait_send()
 
 
-def scratch():
-    shapes = []
+def scratch(held):
+    shapes = [pltpu.VMEM(x.shape, x.dtype) for x in held]
+    shapes += [pltpu.SemaphoreType.DMA((len(held),))]
     shapes += [pltpu.VMEM((9, 40, w), F32) for w in WIDE] * 2
     shapes += [pltpu.VMEM((288, o + e), BF16) for o, e in zip(OWN, EXT)]
     shapes += [pltpu.VMEM((144, o), F32) for o in OWN]
-    shapes += [pltpu.VMEM((144, 9 * 256), BF16), pltpu.VMEM((248, 9 * 256), F32)]
+    shapes += [pltpu.VMEM((144, 9 * 256), BF16)] + [pltpu.VMEM((248, 9 * w), F32) for w in WIDE]
     shapes += [pltpu.VMEM((2, 256, 9 * 256), BF16)]
     shapes += [pltpu.VMEM((o + e, o), BF16) for o, e in zip(OWN, EXT)]
     shapes += [pltpu.VMEM((o, s), BF16) for o, s in zip(OWN, SENT)]
@@ -511,20 +568,21 @@
     place, select, spread = constants()
 
     def on_device(*arrays):
-        consts = (
+        held = arrays[:-1] + (
+            arrays[-1].transpose(1, 0, 2),
             jnp.asarray(place, BF16), jnp.asarray(select, F32), jnp.asarray(spread, BF16),
         )
         return pl.pallas_call(
             functools.partial(kernel, n_dom),
-            out_shape=jax.ShapeDtypeStruct(arrays[0].shape, F32),
-            in_specs=[pl.BlockSpec(memory_space=pltpu.VMEM)] * 13,
+            out_shape=pltpu.VMEM(arrays[0].shape, F32),
+            in_specs=[pl.BlockSpec(memory_space=pltpu.HBM)] * 13,
             out_specs=pl.BlockSpec(memory_space=pltpu.VMEM),
-            scratch_shapes=scratch(),
+            scratch_shapes=scratch(held),
             compiler_params=pltpu.CompilerParams(
                 collective_id=0, has_side_effects=True, vmem_limit_bytes=60 * 1024 * 1024
             ),
             name="step",
-        )(*arrays, *consts)
+        )(*held)
 
     split_all = ("dom", "sub")
     placed = (

time: 48.8 us -> 36.1 us (0.74)
  the two profiles are of different devices: /device:TPU:2 before, /device:TPU:1 now
where the time goes in v2:
time: 36.1 us; the launch traced here: 35.9 us
  Pallas kernels  35 us (97%)
  local copies, waits for them, and re-layouts  0.87 us (2%)
    pallas_call x1, Pallas kernels, on_device(): pl.pallas_call(functools.partial(kernel, n_dom), out_shape=pltpu.VMEM(arr...  35 us
    unnamed x1, local copies, waits for them, and re-layouts  0.87 us

profile of v2, /device:TPU:1, one launch (start us, length us, event | category | flops | bytes accessed | tf_op | source)
XLA Modules:
  0.0 35.9 jit_solution(17267713363717702733)
XLA Ops:
  0.0 35.0 %step.1 = f32[9,35,448]{2,1,0:T(8,128)S(1)} custom-call(f32[9,35,448]{2,1,0:T(8,128)} %refs_0_.1, f32[3,448]{1,0:T(4,128)} %refs_1_.1, f32[3,3,448]{2,1,0:T(4,128)} %refs_2_.1, f32[4,448]{1,0:T(4,128)} %refs_3_.1, f32[3,35,35]{2,1,0:T(8,128)} %refs_4_.1, f32[35,60]{1,0:T(8,128)} %refs_5_.1, s32[4,448]{1,0:T(4,128)} %refs_6_.1, s32[4,448]{1,0:T(4,128)} %refs_7_.1, ...), custom_call_target="tpu_custom_call" | custom-call | tf_op jit(solution)/shard_map/step/pallas_call | solution.py:575
  35.0 0.9 %copy.15 = f32[9,35,448]{2,1,0:T(8,128)} copy(f32[9,35,448]{2,1,0:T(8,128)S(1)} %step.1) | data formatting | bytes 1128960

commit v3 on v2

--- a/solution.py
+++ b/solution.py
@@ -18,7 +18,7 @@
 WIDE = (128, 128, 256)
 OWN = (512, 512, 1024)
 EXT = (128, 256, 384)
-SENT = (128, 256, 384)
+SENT = (128, 256, 256)
 STEP = (COARSE_STEP / 4, COARSE_STEP / 2, COARSE_STEP)
 
 VOIGT = ((3, 8, 7), (8, 4, 6), (7, 6, 5))
@@ -85,10 +85,15 @@
     return pltpu.roll(x, shift, 1) if shift else x
 
 
-def one_hot(rows, base, index):
-    iota = lax.broadcasted_iota(jnp.int32, (rows, index.shape[1]), 0)
-    hit = iota == jnp.broadcast_to(index - base, iota.shape)
-    return jnp.where(hit, 1.0, 0.0).astype(BF16)
+def fill_one_hot(ref, columns, indices, base=0):
+    chunk = 32
+    for start in range(0, ref.shape[0], chunk):
+        iota = lax.broadcasted_iota(jnp.int32, (chunk, indices[0].shape[1]), 0)
+        hit = None
+        for index in indices:
+            here = iota == jnp.broadcast_to(index - (base + start), iota.shape)
+            hit = here if hit is None else hit | here
+        ref[start : start + chunk, columns] = jnp.where(hit, 1.0, 0.0).astype(BF16)
 
 
 def kernel(
@@ -102,15 +107,18 @@
 def body(
     n_dom, ins, in_sems, out,
     wave, mat, geo, fs, der, lift, nbr, ori, halo, iface, place, select, spread,
-    u0, u1, u2, v0, v1, v2, t0, t1, t2, g0, g1, g2, stack, prod0, prod1, prod2, jump,
-    oh0, oh1, oh2, os0, os1, os2, cf0, cf1, cf2, sc0, sc1, sc2, om0, om1, om2,
-    dpad, lpad, amat, lmat, sent0, sent1, sent2, sum_a, sum_b, base0,
-    hs0, hr0, hs1, hr1, hs2, hr2, gs0, gr0, gs1, gr1, gs2, gr2, gs3, gr3,
+    u0, u1, u2, v0, v1, v2, t0, t1, t2, g0, g1, g2,
+    stack0, stack1, stack2, stack3, prod0, prod1, prod2, jump, xj0, xj1, xj2,
+    oh0, oh1, oh2, xx0, xx1, xx2, xm0, xm1, xm2, xs0, xs1, xs2,
+    os0, os1, os2, cf0, cf1, cf2, sc0, sc1, sc2, om0, om1, om2,
+    ix0, ix1, ix2, row_of, xtab, dpad, lpad, amat, smat, emat, lmat, sent0, sent1, sent2, sum_a, sum_b, base0,
+    hs0, hr0, hs1, hr1, hs2, hr2, gs0, gr0, gs1, gr1, gs2, gr2, gs3, gr3, gs4, gr4,
     ss0, rs0, ss1, rs1, ss2, rs2, gss, grs,
 ):
     us, vs, ts, gs_, ohs, oss = (u0, u1, u2), (v0, v1, v2), (t0, t1, t2), (g0, g1, g2), (oh0, oh1, oh2), (os0, os1, os2)
     cfs, scs, oms, sents = (cf0, cf1, cf2), (sc0, sc1, sc2), (om0, om1, om2), (sent0, sent1, sent2)
-    prods = (prod0, prod1, prod2)
+    prods, stacks, xjs = (prod0, prod1, prod2), (stack0, stack1, stack2), (xj0, xj1, xj2)
+    xxs, xms, xss = (xx0, xx1, xx2), (xm0, xm1, xm2), (xs0, xs1, xs2)
     total = n_dom * N_SUB
     dom = lax.axis_index("dom")
     sub = lax.axis_index("sub")
@@ -183,7 +191,7 @@
     halo_c = halo_copies(hs2, hr2, ss2, rs2, 0)
     group = [
         group_copies(s, r, i)
-        for i, (s, r) in enumerate(((gs0, gr0), (gs1, gr1), (gs2, gr2), (gs3, gr3)))
+        for i, (s, r) in enumerate(((gs0, gr0), (gs1, gr1), (gs2, gr2), (gs3, gr3), (gs4, gr4)))
     ]
 
     dpad[...] = jnp.zeros_like(dpad)
@@ -196,7 +204,9 @@
     for k in range(3):
         high, low = split(dpad[k])
         parts.append(dot(high, place[0]) + dot(low, place[1]))
-    amat[...] = jnp.concatenate(parts + [select[...]], axis=0).astype(BF16)
+    amat[...] = jnp.concatenate(parts, axis=0).astype(BF16)
+    smat[...] = select[:, 0:96].astype(BF16)
+    emat[...] = (select[0:64, 0:96] + select[64:128, 0:96]).astype(BF16)
     high, low = split(lpad[...])
     lmat[0:48] = dot(high, spread[...]).astype(BF16)
     lmat[48:96] = dot(low, spread[...]).astype(BF16)
@@ -244,86 +254,99 @@
         elif c == 1:
             rows = [(halo[0:1, 32:96], halo[1:2, 32:96]), (iface[0, 1:2], iface[2, 0:1], blank)]
         else:
-            rows = [
-                (halo[0:1, 96:224],), (halo[1:2, 96:224],), (iface[1, 1:2], iface[2, 1:2], blank),
-            ]
+            rows = [(halo[0:1, 96:224],), (halo[1:2, 96:224],)]
         for i, row in enumerate(rows):
-            index = remap(jnp.concatenate(row, axis=1), c)
-            oss[c][:, 128 * i : 128 * i + 128] = one_hot(OWN[c], 0, index)
+            at = slice(3 * c + i, 3 * c + i + 1)
+            row_of[at] = remap(jnp.concatenate(row, axis=1), c)
+            fill_one_hot(oss[c], slice(128 * i, 128 * i + 128), [row_of[at]])
 
     def neighbour_table(c):
-        span = slice(LANE[c], LANE[c] + WIDE[c])
+        wide, own, ext = WIDE[c], OWN[c], EXT[c]
+        span = slice(LANE[c], LANE[c] + wide)
+        index = remap(nbr[:, span], c)
+        if c == 0:
+            index = jnp.where(lanes(index.shape) < 64, index, -1)
+        ixs = (ix0, ix1, ix2)[c]
+        ixs[...] = jnp.full((8, wide), -1, jnp.int32)
+        ixs[0:4] = index
+        upright = (ixs[...] - own).astype(F32).T
+        across = lanes((32, ext)).astype(F32)
+        scale_at = None
         for f in range(4):
-            where = slice(f * WIDE[c], (f + 1) * WIDE[c])
-            index = remap(nbr[f : f + 1, span], c)
-            ohs[c][:, where] = one_hot(OWN[c] + EXT[c], 0, index)
+            face = slice(f * wide, (f + 1) * wide)
+            fill_one_hot(ohs[c], face, [ixs[f : f + 1]])
+            high, low = split(jnp.broadcast_to(scs[c][:, face], (16, wide)))
+            tall = jnp.concatenate([oms[c][o, :, face] for o in range(3)] + [high, low], axis=0)
+            for start in range(0, wide, 32):
+                column = jnp.broadcast_to(upright[start : start + 32, f : f + 1], (32, ext))
+                xtab[start : start + 32, 0:ext] = jnp.where(column == across, 1.0, 0.0).astype(BF16)
+            found = dot(tall, xtab[0:wide, 0:ext])
+            for o in range(3):
+                xms[c][4 * o + f] = found[16 * o : 16 * o + 16].astype(BF16)
+            both = found[48:64] + found[64:80]
+            scale_at = both if scale_at is None else scale_at + both
+        fill_one_hot(xxs[c], slice(0, wide), [ixs[f : f + 1] for f in range(4)], own)
+        xss[c][...] = scale_at
+
+    def early(c, row):
+        wide = WIDE[c]
+        at = slice(2 * c - 1, 2 * c)
+        row_of[at] = row
+        row = row_of[at]
+        element, face = row & (wide - 1), row >> (7 if c == 1 else 8)
+        tall = jnp.concatenate([us[c][q] for q in range(9)], axis=0)
+        high = tall.astype(BF16).astype(F32)
+        both = jnp.concatenate([high, tall - high], axis=0).astype(BF16)
+        fill_one_hot(xtab.at[0:wide], slice(0, 128), [element])
+        picked = dot(both, xtab[0:wide, 0:128])
+        gap = jnp.zeros((8, 128), F32)
+        for q in range(9):
+            pair = [picked[40 * q : 40 * q + 40], gap, picked[360 + 40 * q : 400 + 40 * q], gap]
+            stack3[:, 128 * q : 128 * q + 128] = jnp.concatenate(pair, axis=0).astype(BF16)
+        nodes = dot(emat[...], stack3[...])
+        face = jnp.broadcast_to(face, (16, 128))
+        found = []
+        for q in range(9):
+            span = slice(128 * q, 128 * q + 128)
+            acc = jnp.zeros((16, 128), F32)
+            for f in range(4):
+                acc = jnp.where(face == f, nodes[16 * f : 16 * f + 16, span], acc)
+            found.append(acc)
+        return jnp.concatenate(found, axis=0)
 
     def traces(c):
         wide = WIDE[c]
-        u, t, prod = us[c], ts[c], prods[c]
+        u, t, stack = us[c], ts[c], stacks[c]
         gap = jnp.zeros((8, wide), F32)
         for q in range(9):
             x = u[q]
             high = x.astype(BF16).astype(F32)
             tall = jnp.concatenate([high, gap, x - high, gap, high, gap], axis=0)
             stack[:, q * wide : (q + 1) * wide] = tall.astype(BF16)
-        span = 9 * wide
-        prod[...] = dot(amat[...], stack[:, 0:span])
+        picked = dot(smat[...], stack[0:96])
         for q in range(9):
             where = slice(q * wide, (q + 1) * wide)
             for part in range(2):
                 for f in range(4):
-                    row = 120 + 64 * part + 16 * f
+                    row = 64 * part + 16 * f
                     t[144 * part + 16 * q : 144 * part + 16 * q + 16, f * wide : (f + 1) * wide] = (
-                        prod[row : row + 16, where].astype(BF16)
+                        picked[row : row + 16, where].astype(BF16)
                     )
-        both = dot(t[:, 0 : OWN[c]], oss[c][...])
+        both = dot(t[...], oss[c][...])
         sents[c][...] = both[0:144] + both[144:288]
 
     def volume(c):
         wide = WIDE[c]
-        cf, prod = cfs[c], prods[c]
-        for start in range(0, wide, 128):
-            span = slice(start, start + 128)
-
-            def grad(q, i, kind):
-                at = q * wide + start
-                base = 9 * kind + 3 * i
-                return sum(
-                    jnp.broadcast_to(cf[base + k : base + k + 1, span], (40, 128))
-                    * prod[40 * k : 40 * k + 40, at : at + 128]
-                    for k in range(3)
-                )
-
-            for i in range(3):
-                rate = grad(VOIGT[i][0], 0, 1) + grad(VOIGT[i][1], 1, 1) + grad(VOIGT[i][2], 2, 1)
-                vs[c][i, :, span] = us[c][i, :, span] + rate
-            diag = [grad(i, i, 2) for i in range(3)]
-            shared = cf[27:28, span] * (diag[0] + diag[1] + diag[2])
-            for i in range(3):
-                vs[c][3 + i, :, span] = us[c][3 + i, :, span] + (shared + cf[28:29, span] * diag[i])
-            for q, i, j in ((6, 1, 2), (7, 0, 2), (8, 0, 1)):
-                rate = grad(j, i, 0) + grad(i, j, 0)
-                vs[c][q, :, span] = us[c][q, :, span] + rate
-        both = dot(ts[c][:, 0 : OWN[c]], ohs[c][0 : OWN[c]])
+        cf, prod, t = cfs[c], prods[c], ts[c]
+        prod[...] = dot(amat[...], stacks[c][...])
+        both = dot(t[...], ohs[c][...])
         gs_[c][...] = both[0:144] + both[144:288]
-
-    def store_ext(c, at, value):
-        high, low = split(value)
-        ts[c][0:144, OWN[c] + at : OWN[c] + at + 128] = high
-        ts[c][144:288, OWN[c] + at : OWN[c] + at + 128] = low
-
-    def finish(c):
-        wide, own = WIDE[c], OWN[c]
-        t = ts[c]
-        both = dot(t[:, own:], ohs[c][own:])
-        gs_[c][...] += both[0:144] + both[144:288]
         scale = scs[c][...]
         for q in range(9):
             rows = slice(16 * q, 16 * q + 16)
             low_rows = slice(144 + 16 * q, 160 + 16 * q)
             high, low = split(gs_[c][rows] * scale)
-            mine = t[rows, 0:own].astype(F32) + t[low_rows, 0:own].astype(F32)
+            mine = t[rows].astype(F32) + t[low_rows].astype(F32)
             own_high, own_low = split(mine * scale)
             where = slice(q * wide, (q + 1) * wide)
             for f in range(4):
@@ -336,12 +359,58 @@
                 at = 192 + 16 * f
                 jump[0, at : at + 16, where] = own_high[:, face]
                 jump[1, at : at + 16, where] = own_low[:, face]
-        span = 9 * wide
-        first = dot(lmat[...], jump[0, :, 0:span])
-        second = dot(lmat[0:48], jump[1, :, 0:span])
+        first = dot(lmat[...], jump[0, :, 0 : 9 * wide])
+        second = dot(lmat[0:48], jump[1, :, 0 : 9 * wide])
         whole = first[0:40] + first[48:88] + second[0:40]
-        for q in range(9):
-            us[c][q] = vs[c][q] + whole[:, q * wide : (q + 1) * wide]
+        for start in range(0, wide, 128):
+            span = slice(start, start + 128)
+
+            def old(q):
+                at = q * wide + start
+                return us[c][q, :, span] + whole[:, at : at + 128]
+
+            def grad(q, i, kind):
+                at = q * wide + start
+                base = 9 * kind + 3 * i
+                return sum(
+                    jnp.broadcast_to(cf[base + k : base + k + 1, span], (40, 128))
+                    * prod[40 * k : 40 * k + 40, at : at + 128]
+                    for k in range(3)
+                )
+
+            for i in range(3):
+                rate = grad(VOIGT[i][0], 0, 1) + grad(VOIGT[i][1], 1, 1) + grad(VOIGT[i][2], 2, 1)
+                vs[c][i, :, span] = old(i) + rate
+            diag = [grad(i, i, 2) for i in range(3)]
+            shared = cf[27:28, span] * (diag[0] + diag[1] + diag[2])
+            for i in range(3):
+                vs[c][3 + i, :, span] = old(3 + i) + (shared + cf[28:29, span] * diag[i])
+            for q, i, j in ((6, 1, 2), (7, 0, 2), (8, 0, 1)):
+                rate = grad(j, i, 0) + grad(i, j, 0)
+                vs[c][q, :, span] = old(q) + rate
+
+    def receive(c, tile, value, new=False):
+        span = slice(128 * tile, 128 * tile + 128)
+        xj = xjs[c]
+        scale = xss[c][:, span]
+        for q in range(9):
+            high, low = split(value[16 * q : 16 * q + 16] * scale)
+            where = slice(128 * q, 128 * q + 128)
+            for i in range(12):
+                mask = xms[c][i, :, span]
+                xj[0, 16 * i : 16 * i + 16, where] = high * mask
+                xj[1, 16 * i : 16 * i + 16, where] = low * mask
+        first = dot(lmat[:, 0:192], xj[0])
+        second = dot(lmat[0:48, 0:192], xj[1])
+        whole = first[0:40] + first[48:88] + second[0:40]
+        tall = jnp.concatenate([whole[:, 128 * q : 128 * q + 128] for q in range(9)], axis=0)
+        high = tall.astype(BF16).astype(F32)
+        both = jnp.concatenate([high, tall - high], axis=0).astype(BF16)
+        added = dot(both, xxs[c][span])
+        target = us[c] if new else vs[c]
+        for q in range(9):
+            at = 40 * q
+            target[q] = vs[c][q] + (added[at : at + 40] + added[360 + at : 400 + at])
 
     lane48 = lanes((48, 128))
     lane16 = lanes((16, 128))
@@ -405,7 +474,7 @@
         pl.when(jnp.logical_not(first))(copies[0].wait_recv)
         pl.when(jnp.logical_not(last))(copies[1].wait_recv)
 
-    def fine_ext(slot):
+    def fine_halo(slot):
         below = hr0[slot, 0]
         above = hr0[slot, 1]
         found = []
@@ -416,15 +485,15 @@
                     jnp.where(lane48 < 64, turn(above, 32 - 32 * r), base0[48 * r : 48 * r + 48]),
                 )
             )
-        store_ext(0, 0, jnp.concatenate(found, axis=0))
-
-    def middle_ext(slot):
+        receive(0, 0, jnp.concatenate(found, axis=0), new=True)
+
+    def middle_halo(slot):
         below = hr1[slot, 0]
         above = hr1[slot, 1]
         left = lanes((80, 128)) < 64
         lower = jnp.where(left, below, turn(above, 64))
         upper = jnp.where(left, turn(below, 64), above)
-        store_ext(1, 0, jnp.concatenate([lower, upper[0:64]], axis=0))
+        receive(1, 0, jnp.concatenate([lower, upper[0:64]], axis=0))
 
     fetched(0, 8, 9)
     load(0)
@@ -435,36 +504,37 @@
     pl.semaphore_wait(barrier, N_SUB - 1 + (me + total - 1) // total + 1 - (me + 1) // total)
     start_halo(halo_f[0])
     load(1)
+    load(2)
+    blank = jnp.full((1, 64), -1, jnp.int32)
+    start_m = early(1, jnp.concatenate([iface[0, 1:2], iface[2, 0:1], blank], axis=1))
+    start_c = early(2, jnp.concatenate([iface[1, 1:2], iface[2, 1:2], blank], axis=1))
+    sum_b[...] = start_m
+    send_group(gs0, gr0, 0, start_m, 0)
+    send_group(gs0, gr0, 1, start_c, 0)
+    start(group[0])
+    send_group(gs4, gr4, 0, start_c, 32)
+    start(group[4])
     send_table(1)
     traces(1)
     send_middle(0)
-    sum_b[...] = sent1[:, 128:256]
-    send_group(gs0, gr0, 0, sent1[:, 128:256], 0)
-    load(2)
+    start_halo(halo_m[0])
     send_table(2)
     traces(2)
-    send_group(gs0, gr0, 1, sent2[:, 256:384], 0)
-    send_group(gs0, gr0, 2, sent2[:, 256:384], 32)
     hs2[0, 0] = sent2[:, 128:256]
     hs2[0, 1] = sent2[:, 0:128]
-    start(group[0])
-    start_halo(halo_m[0])
     start_halo(halo_c)
     fetched(1, 2, 3, 7, 6)
     coefficients(0)
+    neighbour_table(0)
+    volume(0)
     coefficients(1)
     coefficients(2)
-    neighbour_table(0)
-    volume(0)
     neighbour_table(1)
-    volume(1)
     arrive(group[0])
     base0[...] = take_group(gr0, 0, 64) + take_group(gr0, 1, 96)
-    start_mc = take_group(gr0, 2, 32)
 
     arrive_halo(halo_f[0])
-    fine_ext(0)
-    finish(0)
+    fine_halo(0)
     traces(0)
     send_fine(1)
     start_halo(halo_f[1])
@@ -472,13 +542,15 @@
     send_group(gs1, gr1, 0, 0.5 * sum_a[...], 64)
     start(group[1])
     volume(0)
+    volume(1)
+    arrive_halo(halo_m[0])
+    middle_halo(0)
+    arrive(group[4])
+    start_mc = take_group(gr4, 0, 32)
     neighbour_table(2)
-    arrive_halo(halo_m[0])
-    middle_ext(0)
 
     arrive_halo(halo_f[1])
-    fine_ext(1)
-    finish(0)
+    fine_halo(1)
     traces(0)
     send_fine(2)
     start_halo(halo_f[2])
@@ -487,18 +559,16 @@
     volume(0)
 
     arrive(group[1])
-    store_ext(1, 128, take_group(gr1, 0, 0) + start_mc)
-    finish(1)
+    receive(1, 1, take_group(gr1, 0, 0) + start_mc, new=True)
     traces(1)
     send_middle(1)
     start_halo(halo_m[1])
     send_group(gs2, gr2, 0, 0.5 * (sum_b[...] + sent1[:, 128:256]), 32)
     start(group[2])
-    volume(1)
+    volume(2)
 
     arrive_halo(halo_f[2])
-    fine_ext(2)
-    finish(0)
+    fine_halo(2)
     traces(0)
     send_fine(3)
     start_halo(halo_f[3])
@@ -507,22 +577,20 @@
     send_group(gs3, gr3, 1, sum_a[...], 96)
     start(group[3])
     volume(0)
-    volume(2)
+    volume(1)
+    arrive_halo(halo_m[1])
+    middle_halo(1)
     arrive_halo(halo_c)
-    store_ext(2, 0, hr2[0, 0])
-    store_ext(2, 128, hr2[0, 1])
-    arrive_halo(halo_m[1])
-    middle_ext(1)
+    receive(2, 0, hr2[0, 0])
+    receive(2, 1, hr2[0, 1])
+    arrive(group[2])
+    mean = take_group(gr2, 0, 32)
 
     arrive_halo(halo_f[3])
-    fine_ext(3)
-    finish(0)
     arrive(group[3])
-    store_ext(1, 128, take_group(gr3, 0, 0) + start_mc)
-    finish(1)
-    arrive(group[2])
-    store_ext(2, 256, take_group(gr3, 1, 0) + take_group(gr2, 0, 32))
-    finish(2)
+    fine_halo(3)
+    receive(1, 1, take_group(gr3, 0, 0) + start_mc, new=True)
+    receive(2, 2, take_group(gr3, 1, 0) + mean, new=True)
     for q in range(9):
         out[q, :, 0:64] = u0[q, 0:35, 0:64]
         out[q, :, 64:192] = u1[q, 0:35, :]
@@ -539,27 +607,35 @@
     shapes = [pltpu.VMEM(x.shape, x.dtype) for x in held]
     shapes += [pltpu.SemaphoreType.DMA((len(held),))]
     shapes += [pltpu.VMEM((9, 40, w), F32) for w in WIDE] * 2
-    shapes += [pltpu.VMEM((288, o + e), BF16) for o, e in zip(OWN, EXT)]
+    shapes += [pltpu.VMEM((288, o), BF16) for o in OWN]
     shapes += [pltpu.VMEM((144, o), F32) for o in OWN]
-    shapes += [pltpu.VMEM((144, 9 * 256), BF16)] + [pltpu.VMEM((248, 9 * w), F32) for w in WIDE]
+    shapes += [pltpu.VMEM((144, 9 * w), BF16) for w in WIDE] + [pltpu.VMEM((96, 9 * 128), BF16)]
+    shapes += [pltpu.VMEM((120, 9 * w), F32) for w in WIDE]
     shapes += [pltpu.VMEM((2, 256, 9 * 256), BF16)]
-    shapes += [pltpu.VMEM((o + e, o), BF16) for o, e in zip(OWN, EXT)]
+    shapes += [pltpu.VMEM((2, 192, 9 * 128), BF16)] * 3
+    shapes += [pltpu.VMEM((o, o), BF16) for o in OWN]
+    shapes += [pltpu.VMEM((e, w), BF16) for e, w in zip(EXT, WIDE)]
+    shapes += [pltpu.VMEM((12, 16, e), BF16) for e in EXT]
+    shapes += [pltpu.VMEM((16, e), F32) for e in EXT]
     shapes += [pltpu.VMEM((o, s), BF16) for o, s in zip(OWN, SENT)]
     shapes += [pltpu.VMEM((32, w), F32) for w in WIDE]
     shapes += [pltpu.VMEM((1, o), F32) for o in OWN]
     shapes += [pltpu.VMEM((3, 16, o), BF16) for o in OWN]
+    shapes += [pltpu.VMEM((8, w), jnp.int32) for w in WIDE] + [pltpu.VMEM((8, 128), jnp.int32)]
+    shapes += [pltpu.VMEM((256, 384), BF16)]
     shapes += [pltpu.VMEM((3, 40, 128), F32), pltpu.VMEM((48, 128), F32)]
-    shapes += [pltpu.VMEM((248, 144), BF16), pltpu.VMEM((96, 256), BF16)]
+    shapes += [pltpu.VMEM((120, 144), BF16), pltpu.VMEM((128, 96), BF16)]
+    shapes += [pltpu.VMEM((64, 96), BF16), pltpu.VMEM((96, 256), BF16)]
     shapes += [pltpu.VMEM((144, s), F32) for s in SENT]
     shapes += [pltpu.VMEM((144, 128), F32)] * 3
     shapes += [pltpu.VMEM((4, 2, 48, 128), F32)] * 2
     shapes += [pltpu.VMEM((2, 2, 80, 128), F32)] * 2
     shapes += [pltpu.VMEM((1, 2, 144, 128), F32)] * 2
-    for buffers in (3, 1, 1, 2):
+    for buffers in (2, 1, 1, 2, 1):
         shapes += [pltpu.VMEM((N_SUB, 16 * buffers, 128), F32)] * 2
     for slots in (4, 2, 1):
         shapes += [pltpu.SemaphoreType.DMA((slots, 2))] * 2
-    shapes += [pltpu.SemaphoreType.DMA((4, 4))] * 2
+    shapes += [pltpu.SemaphoreType.DMA((5, 4))] * 2
     return shapes
 
 

time: 36.1 us -> 34.7 us (0.961)
  Pallas kernels: 35 us -> 33.7 us
    pallas_call x1, Pallas kernels: 35 us -> 33.7 us  [on_device(): pl.pallas_call(functools.partial(kernel, n_dom), out_shape=pltpu.VMEM(arr...]
where the time goes in v3:
time: 34.7 us; the launch traced here: 34.6 us
  Pallas kernels  33.7 us (97%)
  local copies, waits for them, and re-layouts  0.87 us (3%)
    pallas_call x1, Pallas kernels, on_device(): pl.pallas_call(functools.partial(kernel, n_dom), out_shape=pltpu.VMEM(arr...  33.7 us
    unnamed x1, local copies, waits for them, and re-layouts  0.87 us

profile of v3, /device:TPU:1, one launch (start us, length us, event | category | flops | bytes accessed | tf_op | source)
XLA Modules:
  0.0 34.6 jit_solution(7753765334434525495)
XLA Ops:
  0.0 33.7 %step.1 = f32[9,35,448]{2,1,0:T(8,128)S(1)} custom-call(f32[9,35,448]{2,1,0:T(8,128)} %refs_0_.1, f32[3,448]{1,0:T(4,128)} %refs_1_.1, f32[3,3,448]{2,1,0:T(4,128)} %refs_2_.1, f32[4,448]{1,0:T(4,128)} %refs_3_.1, f32[3,35,35]{2,1,0:T(8,128)} %refs_4_.1, f32[35,60]{1,0:T(8,128)} %refs_5_.1, s32[4,448]{1,0:T(4,128)} %refs_6_.1, s32[4,448]{1,0:T(4,128)} %refs_7_.1, ...), custom_call_target="tpu_custom_call" | custom-call | tf_op jit(solution)/shard_map/step/pallas_call | solution.py:651
  33.7 0.9 %copy.15 = f32[9,35,448]{2,1,0:T(8,128)} copy(f32[9,35,448]{2,1,0:T(8,128)S(1)} %step.1) | data formatting | bytes 1128960

commit v4 on v3

--- a/solution.py
+++ b/solution.py
@@ -58,13 +58,15 @@
         for n in range(15):
             select[f * 16 + n, face_rows[f, n]] = 1
             select[64 + f * 16 + n, 48 + face_rows[f, n]] = 1
-    spread = np.zeros((128, 256), np.float32)
+    spread = np.zeros((2, 128, 128), np.float32)
     for f in range(4):
         for n in range(15):
-            for o in range(3):
-                spread[f * 15 + n, (o * 4 + f) * 16 + orders[o, n]] = 1
-            spread[f * 15 + n, 192 + f * 16 + n] = -1
-    return place, select, spread
+            spread[0, f * 15 + n, f * 16 + n] = 1
+            spread[0, f * 15 + n, 64 + f * 16 + n] = 1
+            spread[1, f * 15 + n, f * 16 + n] = 1
+    turns = np.full((3, 16, 128), 15, np.int32)
+    turns[:, :15] = orders[:, :, None]
+    return place, select, spread, turns
 
 
 def split(x):
@@ -85,31 +87,42 @@
     return pltpu.roll(x, shift, 1) if shift else x
 
 
-def fill_one_hot(ref, columns, indices, base=0):
+def put(ref, rows, tile, value):
+    for i in range(value.shape[1] // 128):
+        ref[tile + i, rows, :] = value[:, 128 * i : 128 * i + 128]
+
+
+def get(ref, rows=slice(None), start=0, stop=None):
+    stop = ref.shape[0] if stop is None else stop
+    return jnp.concatenate([ref[i, rows, :] for i in range(start, stop)], axis=1)
+
+
+def fill_one_hot(ref, tile, indices, base=0, rows=None):
     chunk = 32
-    for start in range(0, ref.shape[0], chunk):
+    for start in range(0, rows or ref.shape[1], chunk):
         iota = lax.broadcasted_iota(jnp.int32, (chunk, indices[0].shape[1]), 0)
         hit = None
         for index in indices:
             here = iota == jnp.broadcast_to(index - (base + start), iota.shape)
             hit = here if hit is None else hit | here
-        ref[start : start + chunk, columns] = jnp.where(hit, 1.0, 0.0).astype(BF16)
+        put(ref, slice(start, start + chunk), tile, jnp.where(hit, 1.0, 0.0).astype(BF16))
 
 
 def kernel(
     n_dom,
     *refs,
 ):
-    ins, out, held, in_sems, rest = refs[:13], refs[13], refs[14:27], refs[27], refs[28:]
+    ins, out, held, in_sems, rest = refs[:14], refs[14], refs[15:29], refs[29], refs[30:]
     body(n_dom, ins, in_sems, out, *held, *rest)
 
 
 def body(
     n_dom, ins, in_sems, out,
-    wave, mat, geo, fs, der, lift, nbr, ori, halo, iface, place, select, spread,
+    wave, mat, geo, fs, der, lift, nbr, ori, halo, iface, place, select, spread, turns,
     u0, u1, u2, v0, v1, v2, t0, t1, t2, g0, g1, g2,
     stack0, stack1, stack2, stack3, prod0, prod1, prod2, jump, xj0, xj1, xj2,
     oh0, oh1, oh2, xx0, xx1, xx2, xm0, xm1, xm2, xs0, xs1, xs2,
+    xi0, xi1, xi2, tn0, tn1, tn2,
     os0, os1, os2, cf0, cf1, cf2, sc0, sc1, sc2, om0, om1, om2,
     ix0, ix1, ix2, row_of, xtab, dpad, lpad, amat, smat, emat, lmat, sent0, sent1, sent2, sum_a, sum_b, base0,
     hs0, hr0, hs1, hr1, hs2, hr2, gs0, gr0, gs1, gr1, gs2, gr2, gs3, gr3, gs4, gr4,
@@ -118,6 +131,7 @@
     us, vs, ts, gs_, ohs, oss = (u0, u1, u2), (v0, v1, v2), (t0, t1, t2), (g0, g1, g2), (oh0, oh1, oh2), (os0, os1, os2)
     cfs, scs, oms, sents = (cf0, cf1, cf2), (sc0, sc1, sc2), (om0, om1, om2), (sent0, sent1, sent2)
     prods, stacks, xjs = (prod0, prod1, prod2), (stack0, stack1, stack2), (xj0, xj1, xj2)
+    xis, turn_of = (xi0, xi1, xi2), (tn0, tn1, tn2)
     xxs, xms, xss = (xx0, xx1, xx2), (xm0, xm1, xm2), (xs0, xs1, xs2)
     total = n_dom * N_SUB
     dom = lax.axis_index("dom")
@@ -167,10 +181,10 @@
             )
         return found
 
-    held = (wave, mat, geo, fs, der, lift, nbr, ori, halo, iface, place, select, spread)
+    held = (wave, mat, geo, fs, der, lift, nbr, ori, halo, iface, place, select, spread, turns)
     fetch = {
         i: pltpu.make_async_copy(ins[i], held[i], in_sems.at[i])
-        for i in (4, 5, 10, 11, 12, 0, 8, 9, 1, 2, 3, 7, 6)
+        for i in (4, 5, 10, 11, 12, 0, 8, 9, 1, 2, 3, 7, 6, 13)
     }
     for copy in fetch.values():
         copy.start()
@@ -208,8 +222,8 @@
     smat[...] = select[:, 0:96].astype(BF16)
     emat[...] = (select[0:64, 0:96] + select[64:128, 0:96]).astype(BF16)
     high, low = split(lpad[...])
-    lmat[0:48] = dot(high, spread[...]).astype(BF16)
-    lmat[48:96] = dot(low, spread[...]).astype(BF16)
+    lmat[0:48] = dot(high, spread[0]).astype(BF16)
+    lmat[48:96] = dot(low, spread[1]).astype(BF16)
 
     def remap(index, c):
         if c:
@@ -217,6 +231,18 @@
         return jnp.where(
             index < 256, (index & 63) + ((index >> 6) << 7), index + 256
         )
+
+    def order_of(turned):
+        return jnp.where(turned == 0, turns[0], jnp.where(turned == 1, turns[1], turns[2]))
+
+    def reorder(x, order):
+        found = []
+        for half in (order[0:8], order[8:16]):
+            row = half & 7
+            low = jnp.take_along_axis(x[0:8], row, axis=0, mode="promise_in_bounds")
+            high = jnp.take_along_axis(x[8:16], row, axis=0, mode="promise_in_bounds")
+            found.append(jnp.where(half < 8, low, high))
+        return jnp.concatenate(found, axis=0)
 
     def load(c):
         first, wide = LANE[c], WIDE[c]
@@ -243,9 +269,11 @@
         for f in range(4):
             where = slice(f * wide, (f + 1) * wide)
             scs[c][:, where] = (0.5 * STEP[c]) * fs[f : f + 1, span]
-            row = jnp.broadcast_to(ori[f : f + 1, span], (16, wide))
-            for o in range(3):
-                oms[c][o, :, where] = jnp.where(row == o, 1.0, 0.0).astype(BF16)
+            turn_of[c][f : f + 1] = ori[f : f + 1, span]
+            for j in range(wide // 128):
+                oms[c][f * wide // 128 + j] = order_of(
+                    jnp.broadcast_to(turn_of[c][f : f + 1, 128 * j : 128 * j + 128], (16, 128))
+                )
 
     def send_table(c):
         blank = jnp.full((1, 64), -1, jnp.int32)
@@ -258,7 +286,7 @@
         for i, row in enumerate(rows):
             at = slice(3 * c + i, 3 * c + i + 1)
             row_of[at] = remap(jnp.concatenate(row, axis=1), c)
-            fill_one_hot(oss[c], slice(128 * i, 128 * i + 128), [row_of[at]])
+            fill_one_hot(oss[c], i, [row_of[at]])
 
     def neighbour_table(c):
         wide, own, ext = WIDE[c], OWN[c], EXT[c]
@@ -271,21 +299,24 @@
         ixs[0:4] = index
         upright = (ixs[...] - own).astype(F32).T
         across = lanes((32, ext)).astype(F32)
-        scale_at = None
+        scale_at, turned_at = None, None
         for f in range(4):
             face = slice(f * wide, (f + 1) * wide)
-            fill_one_hot(ohs[c], face, [ixs[f : f + 1]])
+            fill_one_hot(ohs[c], f * wide // 128, [ixs[f : f + 1]])
             high, low = split(jnp.broadcast_to(scs[c][:, face], (16, wide)))
-            tall = jnp.concatenate([oms[c][o, :, face] for o in range(3)] + [high, low], axis=0)
+            turned = jnp.broadcast_to(turn_of[c][f : f + 1].astype(F32), (16, wide)).astype(BF16)
+            tall = jnp.concatenate([turned, jnp.ones((16, wide), BF16), high, low], axis=0)
             for start in range(0, wide, 32):
                 column = jnp.broadcast_to(upright[start : start + 32, f : f + 1], (32, ext))
-                xtab[start : start + 32, 0:ext] = jnp.where(column == across, 1.0, 0.0).astype(BF16)
-            found = dot(tall, xtab[0:wide, 0:ext])
-            for o in range(3):
-                xms[c][4 * o + f] = found[16 * o : 16 * o + 16].astype(BF16)
-            both = found[48:64] + found[64:80]
+                put(xtab, slice(start, start + 32), 0, jnp.where(column == across, 1.0, 0.0).astype(BF16))
+            found = dot(tall, get(xtab, slice(0, wide), 0, ext // 128))
+            put(xms[c].at[f], slice(None), 0, found[16:32].astype(BF16))
+            both = found[32:48] + found[48:64]
             scale_at = both if scale_at is None else scale_at + both
-        fill_one_hot(xxs[c], slice(0, wide), [ixs[f : f + 1] for f in range(4)], own)
+            turned_at = found[0:16] if turned_at is None else turned_at + found[0:16]
+        for i in range(ext // 128):
+            xis[c][i] = order_of(turned_at[:, 128 * i : 128 * i + 128].astype(jnp.int32))
+        fill_one_hot(xxs[c], 0, [ixs[f : f + 1] for f in range(4)], own)
         xss[c][...] = scale_at
 
     def early(c, row):
@@ -297,13 +328,13 @@
         tall = jnp.concatenate([us[c][q] for q in range(9)], axis=0)
         high = tall.astype(BF16).astype(F32)
         both = jnp.concatenate([high, tall - high], axis=0).astype(BF16)
-        fill_one_hot(xtab.at[0:wide], slice(0, 128), [element])
-        picked = dot(both, xtab[0:wide, 0:128])
+        fill_one_hot(xtab, 0, [element], rows=wide)
+        picked = dot(both, xtab[0, 0:wide])
         gap = jnp.zeros((8, 128), F32)
         for q in range(9):
             pair = [picked[40 * q : 40 * q + 40], gap, picked[360 + 40 * q : 400 + 40 * q], gap]
-            stack3[:, 128 * q : 128 * q + 128] = jnp.concatenate(pair, axis=0).astype(BF16)
-        nodes = dot(emat[...], stack3[...])
+            stack3[q] = jnp.concatenate(pair, axis=0).astype(BF16)
+        nodes = dot(emat[...], get(stack3))
         face = jnp.broadcast_to(face, (16, 128))
         found = []
         for q in range(9):
@@ -322,46 +353,40 @@
             x = u[q]
             high = x.astype(BF16).astype(F32)
             tall = jnp.concatenate([high, gap, x - high, gap, high, gap], axis=0)
-            stack[:, q * wide : (q + 1) * wide] = tall.astype(BF16)
-        picked = dot(smat[...], stack[0:96])
+            put(stack, slice(None), q * wide // 128, tall.astype(BF16))
+        picked = dot(smat[...], get(stack, slice(0, 96)))
         for q in range(9):
             where = slice(q * wide, (q + 1) * wide)
             for part in range(2):
                 for f in range(4):
                     row = 64 * part + 16 * f
-                    t[144 * part + 16 * q : 144 * part + 16 * q + 16, f * wide : (f + 1) * wide] = (
-                        picked[row : row + 16, where].astype(BF16)
-                    )
-        both = dot(t[...], oss[c][...])
+                    at = 144 * part + 16 * q
+                    value = picked[row : row + 16, where].astype(BF16)
+                    put(t, slice(at, at + 16), f * wide // 128, value)
+        both = dot(get(t), get(oss[c]))
         sents[c][...] = both[0:144] + both[144:288]
 
     def volume(c):
         wide = WIDE[c]
         cf, prod, t = cfs[c], prods[c], ts[c]
-        prod[...] = dot(amat[...], stacks[c][...])
-        both = dot(t[...], ohs[c][...])
+        tiles, own_tiles = wide // 128, OWN[c] // 128
+        prod[...] = dot(amat[...], get(stacks[c]))
+        both = dot(get(t), get(ohs[c]))
         gs_[c][...] = both[0:144] + both[144:288]
         scale = scs[c][...]
-        for q in range(9):
-            rows = slice(16 * q, 16 * q + 16)
-            low_rows = slice(144 + 16 * q, 160 + 16 * q)
-            high, low = split(gs_[c][rows] * scale)
-            mine = t[rows].astype(F32) + t[low_rows].astype(F32)
-            own_high, own_low = split(mine * scale)
-            where = slice(q * wide, (q + 1) * wide)
-            for f in range(4):
-                face = slice(f * wide, (f + 1) * wide)
-                for o in range(3):
-                    mask = oms[c][o, :, face]
-                    at = (4 * o + f) * 16
-                    jump[0, at : at + 16, where] = high[:, face] * mask
-                    jump[1, at : at + 16, where] = low[:, face] * mask
-                at = 192 + 16 * f
-                jump[0, at : at + 16, where] = own_high[:, face]
-                jump[1, at : at + 16, where] = own_low[:, face]
-        first = dot(lmat[...], jump[0, :, 0 : 9 * wide])
-        second = dot(lmat[0:48], jump[1, :, 0 : 9 * wide])
-        whole = first[0:40] + first[48:88] + second[0:40]
+        for j in range(own_tiles):
+            lane = slice(128 * j, 128 * j + 128)
+            f, part = j // tiles, j % tiles
+            order = oms[c][j]
+            for q in range(9):
+                at = 16 * q
+                outer = reorder(gs_[c][at : at + 16, lane], order)
+                mine = t[j, at : at + 16].astype(F32) + t[j, 144 + at : 160 + at].astype(F32)
+                high, low = split((outer - mine) * scale[:, lane])
+                jump[q * tiles + part, 16 * f : 16 * f + 16] = high
+                jump[q * tiles + part, 64 + 16 * f : 80 + 16 * f] = low
+        first = dot(lmat[...], get(jump, slice(None), 0, 9 * tiles))
+        whole = first[0:40] + first[48:88]
         for start in range(0, wide, 128):
             span = slice(start, start + 128)
 
@@ -392,21 +417,19 @@
     def receive(c, tile, value, new=False):
         span = slice(128 * tile, 128 * tile + 128)
         xj = xjs[c]
-        scale = xss[c][:, span]
-        for q in range(9):
-            high, low = split(value[16 * q : 16 * q + 16] * scale)
-            where = slice(128 * q, 128 * q + 128)
-            for i in range(12):
-                mask = xms[c][i, :, span]
-                xj[0, 16 * i : 16 * i + 16, where] = high * mask
-                xj[1, 16 * i : 16 * i + 16, where] = low * mask
-        first = dot(lmat[:, 0:192], xj[0])
-        second = dot(lmat[0:48, 0:192], xj[1])
-        whole = first[0:40] + first[48:88] + second[0:40]
+        scale, order = xss[c][:, span], xis[c][tile]
+        for q in range(9):
+            high, low = split(reorder(value[16 * q : 16 * q + 16], order) * scale)
+            for f in range(4):
+                mask = xms[c][f, tile]
+                xj[q, 16 * f : 16 * f + 16] = high * mask
+                xj[q, 64 + 16 * f : 80 + 16 * f] = low * mask
+        first = dot(lmat[...], get(xj))
+        whole = first[0:40] + first[48:88]
         tall = jnp.concatenate([whole[:, 128 * q : 128 * q + 128] for q in range(9)], axis=0)
         high = tall.astype(BF16).astype(F32)
         both = jnp.concatenate([high, tall - high], axis=0).astype(BF16)
-        added = dot(both, xxs[c][span])
+        added = dot(both, get(xxs[c], span))
         target = us[c] if new else vs[c]
         for q in range(9):
             at = 40 * q
@@ -523,7 +546,7 @@
     hs2[0, 0] = sent2[:, 128:256]
     hs2[0, 1] = sent2[:, 0:128]
     start_halo(halo_c)
-    fetched(1, 2, 3, 7, 6)
+    fetched(1, 2, 3, 7, 6, 13)
     coefficients(0)
     neighbour_table(0)
     volume(0)
@@ -607,25 +630,28 @@
     shapes = [pltpu.VMEM(x.shape, x.dtype) for x in held]
     shapes += [pltpu.SemaphoreType.DMA((len(held),))]
     shapes += [pltpu.VMEM((9, 40, w), F32) for w in WIDE] * 2
-    shapes += [pltpu.VMEM((288, o), BF16) for o in OWN]
+    shapes += [pltpu.VMEM((o // 128, 288, 128), BF16) for o in OWN]
     shapes += [pltpu.VMEM((144, o), F32) for o in OWN]
-    shapes += [pltpu.VMEM((144, 9 * w), BF16) for w in WIDE] + [pltpu.VMEM((96, 9 * 128), BF16)]
+    shapes += [pltpu.VMEM((9 * w // 128, 144, 128), BF16) for w in WIDE]
+    shapes += [pltpu.VMEM((9, 96, 128), BF16)]
     shapes += [pltpu.VMEM((120, 9 * w), F32) for w in WIDE]
-    shapes += [pltpu.VMEM((2, 256, 9 * 256), BF16)]
-    shapes += [pltpu.VMEM((2, 192, 9 * 128), BF16)] * 3
-    shapes += [pltpu.VMEM((o, o), BF16) for o in OWN]
-    shapes += [pltpu.VMEM((e, w), BF16) for e, w in zip(EXT, WIDE)]
-    shapes += [pltpu.VMEM((12, 16, e), BF16) for e in EXT]
+    shapes += [pltpu.VMEM((18, 128, 128), BF16)]
+    shapes += [pltpu.VMEM((9, 128, 128), BF16)] * 3
+    shapes += [pltpu.VMEM((o // 128, o, 128), BF16) for o in OWN]
+    shapes += [pltpu.VMEM((w // 128, e, 128), BF16) for e, w in zip(EXT, WIDE)]
+    shapes += [pltpu.VMEM((4, e // 128, 16, 128), BF16) for e in EXT]
     shapes += [pltpu.VMEM((16, e), F32) for e in EXT]
-    shapes += [pltpu.VMEM((o, s), BF16) for o, s in zip(OWN, SENT)]
+    shapes += [pltpu.VMEM((e // 128, 16, 128), jnp.int32) for e in EXT]
+    shapes += [pltpu.VMEM((8, w), jnp.int32) for w in WIDE]
+    shapes += [pltpu.VMEM((s // 128, o, 128), BF16) for o, s in zip(OWN, SENT)]
     shapes += [pltpu.VMEM((32, w), F32) for w in WIDE]
     shapes += [pltpu.VMEM((1, o), F32) for o in OWN]
-    shapes += [pltpu.VMEM((3, 16, o), BF16) for o in OWN]
+    shapes += [pltpu.VMEM((o // 128, 16, 128), jnp.int32) for o in OWN]
     shapes += [pltpu.VMEM((8, w), jnp.int32) for w in WIDE] + [pltpu.VMEM((8, 128), jnp.int32)]
-    shapes += [pltpu.VMEM((256, 384), BF16)]
+    shapes += [pltpu.VMEM((3, 256, 128), BF16)]
     shapes += [pltpu.VMEM((3, 40, 128), F32), pltpu.VMEM((48, 128), F32)]
     shapes += [pltpu.VMEM((120, 144), BF16), pltpu.VMEM((128, 96), BF16)]
-    shapes += [pltpu.VMEM((64, 96), BF16), pltpu.VMEM((96, 256), BF16)]
+    shapes += [pltpu.VMEM((64, 96), BF16), pltpu.VMEM((96, 128), BF16)]
     shapes += [pltpu.VMEM((144, s), F32) for s in SENT]
     shapes += [pltpu.VMEM((144, 128), F32)] * 3
     shapes += [pltpu.VMEM((4, 2, 48, 128), F32)] * 2
@@ -641,17 +667,18 @@
 
 def solution(mesh):
     n_dom = mesh.shape["dom"]
-    place, select, spread = constants()
+    place, select, spread, turns = constants()
 
     def on_device(*arrays):
         held = arrays[:-1] + (
             arrays[-1].transpose(1, 0, 2),
             jnp.asarray(place, BF16), jnp.asarray(select, F32), jnp.asarray(spread, BF16),
+            jnp.asarray(turns),
         )
         return pl.pallas_call(
             functools.partial(kernel, n_dom),
             out_shape=pltpu.VMEM(arrays[0].shape, F32),
-            in_specs=[pl.BlockSpec(memory_space=pltpu.HBM)] * 13,
+            in_specs=[pl.BlockSpec(memory_space=pltpu.HBM)] * 14,
             out_specs=pl.BlockSpec(memory_space=pltpu.VMEM),
             scratch_shapes=scratch(held),
             compiler_params=pltpu.CompilerParams(

time: 34.7 us -> 33.6 us (0.968)
  the two profiles are of different devices: /device:TPU:1 before, /device:TPU:512 now
where the time goes in v4:
time: 33.6 us; the launch traced here: 33.4 us
  Pallas kernels  32.6 us (97%)
  local copies, waits for them, and re-layouts  0.87 us (3%)
    pallas_call x1, Pallas kernels, on_device(): pl.pallas_call(functools.partial(kernel, n_dom), out_shape=pltpu.VMEM(arr...  32.6 us
    unnamed x1, local copies, waits for them, and re-layouts  0.87 us

profile of v4, /device:TPU:512, one launch (start us, length us, event | category | flops | bytes accessed | tf_op | source)
XLA Modules:
  0.0 33.4 jit_solution(10740544834051891144)
XLA Ops:
  0.0 32.6 %step.1 = f32[9,35,448]{2,1,0:T(8,128)S(1)} custom-call(f32[9,35,448]{2,1,0:T(8,128)} %refs_0_.1, f32[3,448]{1,0:T(4,128)} %refs_1_.1, f32[3,3,448]{2,1,0:T(4,128)} %refs_2_.1, f32[4,448]{1,0:T(4,128)} %refs_3_.1, f32[3,35,35]{2,1,0:T(8,128)} %refs_4_.1, f32[35,60]{1,0:T(8,128)} %refs_5_.1, s32[4,448]{1,0:T(4,128)} %refs_6_.1, s32[4,448]{1,0:T(4,128)} %refs_7_.1, ...), custom_call_target="tpu_custom_call" | custom-call | tf_op jit(solution)/shard_map/step/pallas_call | solution.py:678
  32.6 0.9 %copy.16 = f32[9,35,448]{2,1,0:T(8,128)} copy(f32[9,35,448]{2,1,0:T(8,128)S(1)} %step.1) | data formatting | bytes 1128960

commit v5 on v4

--- a/solution.py
+++ b/solution.py
@@ -124,7 +124,7 @@
     oh0, oh1, oh2, xx0, xx1, xx2, xm0, xm1, xm2, xs0, xs1, xs2,
     xi0, xi1, xi2, tn0, tn1, tn2,
     os0, os1, os2, cf0, cf1, cf2, sc0, sc1, sc2, om0, om1, om2,
-    ix0, ix1, ix2, row_of, xtab, dpad, lpad, amat, smat, emat, lmat, sent0, sent1, sent2, sum_a, sum_b, base0,
+    ix0, ix1, ix2, row_of, xtab, dpad, lpad, amat, emat, lmat, sent0, sent1, sent2, sum_a, sum_b, base0,
     hs0, hr0, hs1, hr1, hs2, hr2, gs0, gr0, gs1, gr1, gs2, gr2, gs3, gr3, gs4, gr4,
     ss0, rs0, ss1, rs1, ss2, rs2, gss, grs,
 ):
@@ -219,7 +219,6 @@
         high, low = split(dpad[k])
         parts.append(dot(high, place[0]) + dot(low, place[1]))
     amat[...] = jnp.concatenate(parts, axis=0).astype(BF16)
-    smat[...] = select[:, 0:96].astype(BF16)
     emat[...] = (select[0:64, 0:96] + select[64:128, 0:96]).astype(BF16)
     high, low = split(lpad[...])
     lmat[0:48] = dot(high, spread[0]).astype(BF16)
@@ -289,7 +288,7 @@
             fill_one_hot(oss[c], i, [row_of[at]])
 
     def neighbour_table(c):
-        wide, own, ext = WIDE[c], OWN[c], EXT[c]
+        wide, own = WIDE[c], OWN[c]
         span = slice(LANE[c], LANE[c] + wide)
         index = remap(nbr[:, span], c)
         if c == 0:
@@ -297,12 +296,17 @@
         ixs = (ix0, ix1, ix2)[c]
         ixs[...] = jnp.full((8, wide), -1, jnp.int32)
         ixs[0:4] = index
+        for f in range(4):
+            fill_one_hot(ohs[c], f * wide // 128, [ixs[f : f + 1]])
+
+    def received_table(c):
+        wide, own, ext = WIDE[c], OWN[c], EXT[c]
+        ixs = (ix0, ix1, ix2)[c]
         upright = (ixs[...] - own).astype(F32).T
         across = lanes((32, ext)).astype(F32)
         scale_at, turned_at = None, None
         for f in range(4):
             face = slice(f * wide, (f + 1) * wide)
-            fill_one_hot(ohs[c], f * wide // 128, [ixs[f : f + 1]])
             high, low = split(jnp.broadcast_to(scs[c][:, face], (16, wide)))
             turned = jnp.broadcast_to(turn_of[c][f : f + 1].astype(F32), (16, wide)).astype(BF16)
             tall = jnp.concatenate([turned, jnp.ones((16, wide), BF16), high, low], axis=0)
@@ -354,15 +358,14 @@
             high = x.astype(BF16).astype(F32)
             tall = jnp.concatenate([high, gap, x - high, gap, high, gap], axis=0)
             put(stack, slice(None), q * wide // 128, tall.astype(BF16))
-        picked = dot(smat[...], get(stack, slice(0, 96)))
+        picked = dot(emat[...], get(stack, slice(0, 96)))
         for q in range(9):
             where = slice(q * wide, (q + 1) * wide)
-            for part in range(2):
-                for f in range(4):
-                    row = 64 * part + 16 * f
-                    at = 144 * part + 16 * q
-                    value = picked[row : row + 16, where].astype(BF16)
-                    put(t, slice(at, at + 16), f * wide // 128, value)
+            for f in range(4):
+                at, tile = 16 * q, f * wide // 128
+                high, low = split(picked[16 * f : 16 * f + 16, where])
+                put(t, slice(at, at + 16), tile, high)
+                put(t, slice(144 + at, 160 + at), tile, low)
         both = dot(get(t), get(oss[c]))
         sents[c][...] = both[0:144] + both[144:288]
 
@@ -428,12 +431,13 @@
         whole = first[0:40] + first[48:88]
         tall = jnp.concatenate([whole[:, 128 * q : 128 * q + 128] for q in range(9)], axis=0)
         high = tall.astype(BF16).astype(F32)
-        both = jnp.concatenate([high, tall - high], axis=0).astype(BF16)
-        added = dot(both, get(xxs[c], span))
+        both = jnp.concatenate([high, tall - high], axis=1).astype(BF16)
+        columns = get(xxs[c], span)
+        added = dot(both, jnp.concatenate([columns, columns], axis=0))
         target = us[c] if new else vs[c]
         for q in range(9):
             at = 40 * q
-            target[q] = vs[c][q] + (added[at : at + 40] + added[360 + at : 400 + at])
+            target[q] = vs[c][q] + added[at : at + 40]
 
     lane48 = lanes((48, 128))
     lane16 = lanes((16, 128))
@@ -549,10 +553,12 @@
     fetched(1, 2, 3, 7, 6, 13)
     coefficients(0)
     neighbour_table(0)
+    received_table(0)
     volume(0)
     coefficients(1)
     coefficients(2)
     neighbour_table(1)
+    received_table(1)
     arrive(group[0])
     base0[...] = take_group(gr0, 0, 64) + take_group(gr0, 1, 96)
 
@@ -601,6 +607,7 @@
     start(group[3])
     volume(0)
     volume(1)
+    received_table(2)
     arrive_halo(halo_m[1])
     middle_halo(1)
     arrive_halo(halo_c)
@@ -650,7 +657,7 @@
     shapes += [pltpu.VMEM((8, w), jnp.int32) for w in WIDE] + [pltpu.VMEM((8, 128), jnp.int32)]
     shapes += [pltpu.VMEM((3, 256, 128), BF16)]
     shapes += [pltpu.VMEM((3, 40, 128), F32), pltpu.VMEM((48, 128), F32)]
-    shapes += [pltpu.VMEM((120, 144), BF16), pltpu.VMEM((128, 96), BF16)]
+    shapes += [pltpu.VMEM((120, 144), BF16)]
     shapes += [pltpu.VMEM((64, 96), BF16), pltpu.VMEM((96, 128), BF16)]
     shapes += [pltpu.VMEM((144, s), F32) for s in SENT]
     shapes += [pltpu.VMEM((144, 128), F32)] * 3

time: 33.6 us -> 33 us (0.982)
  Pallas kernels: 32.6 us -> 31.9 us
    pallas_call x1, Pallas kernels: 32.6 us -> 31.9 us  [on_device(): pl.pallas_call(functools.partial(kernel, n_dom), out_shape=pltpu.VMEM(arr...]
where the time goes in v5:
time: 33 us; the launch traced here: 32.8 us
  Pallas kernels  31.9 us (97%)
  local copies, waits for them, and re-layouts  0.87 us (3%)
    pallas_call x1, Pallas kernels, on_device(): pl.pallas_call(functools.partial(kernel, n_dom), out_shape=pltpu.VMEM(arr...  31.9 us
    unnamed x1, local copies, waits for them, and re-layouts  0.87 us

profile of v5, /device:TPU:512, one launch (start us, length us, event | category | flops | bytes accessed | tf_op | source)
XLA Modules:
  0.0 32.8 jit_solution(3236029856020672712)
XLA Ops:
  0.0 31.9 %step.1 = f32[9,35,448]{2,1,0:T(8,128)S(1)} custom-call(f32[9,35,448]{2,1,0:T(8,128)} %refs_0_.1, f32[3,448]{1,0:T(4,128)} %refs_1_.1, f32[3,3,448]{2,1,0:T(4,128)} %refs_2_.1, f32[4,448]{1,0:T(4,128)} %refs_3_.1, f32[3,35,35]{2,1,0:T(8,128)} %refs_4_.1, f32[35,60]{1,0:T(8,128)} %refs_5_.1, s32[4,448]{1,0:T(4,128)} %refs_6_.1, s32[4,448]{1,0:T(4,128)} %refs_7_.1, ...), custom_call_target="tpu_custom_call" | custom-call | tf_op jit(solution)/shard_map/step/pallas_call | solution.py:685
  31.9 0.9 %copy.16 = f32[9,35,448]{2,1,0:T(8,128)} copy(f32[9,35,448]{2,1,0:T(8,128)S(1)} %step.1) | data formatting | bytes 1128960

commit v6 on v5

--- a/solution.py
+++ b/solution.py
@@ -184,7 +184,7 @@
     held = (wave, mat, geo, fs, der, lift, nbr, ori, halo, iface, place, select, spread, turns)
     fetch = {
         i: pltpu.make_async_copy(ins[i], held[i], in_sems.at[i])
-        for i in (4, 5, 10, 11, 12, 0, 8, 9, 1, 2, 3, 7, 6, 13)
+        for i in (11, 0, 8, 9, 4, 5, 10, 12, 1, 2, 3, 7, 6, 13)
     }
     for copy in fetch.values():
         copy.start()
@@ -208,21 +208,24 @@
         for i, (s, r) in enumerate(((gs0, gr0), (gs1, gr1), (gs2, gr2), (gs3, gr3), (gs4, gr4)))
     ]
 
-    dpad[...] = jnp.zeros_like(dpad)
-    lpad[...] = jnp.zeros_like(lpad)
-    fetched(4, 5, 10, 11, 12)
-    for k in range(3):
-        dpad[k, 0:35, 0:35] = der[k]
-    lpad[0:35, 0:60] = lift[...]
-    parts = []
-    for k in range(3):
-        high, low = split(dpad[k])
-        parts.append(dot(high, place[0]) + dot(low, place[1]))
-    amat[...] = jnp.concatenate(parts, axis=0).astype(BF16)
+    fetched(11)
     emat[...] = (select[0:64, 0:96] + select[64:128, 0:96]).astype(BF16)
-    high, low = split(lpad[...])
-    lmat[0:48] = dot(high, spread[0]).astype(BF16)
-    lmat[48:96] = dot(low, spread[1]).astype(BF16)
+
+    def matrices():
+        dpad[...] = jnp.zeros_like(dpad)
+        lpad[...] = jnp.zeros_like(lpad)
+        fetched(4, 5, 10, 12)
+        for k in range(3):
+            dpad[k, 0:35, 0:35] = der[k]
+        lpad[0:35, 0:60] = lift[...]
+        parts = []
+        for k in range(3):
+            high, low = split(dpad[k])
+            parts.append(dot(high, place[0]) + dot(low, place[1]))
+        amat[...] = jnp.concatenate(parts, axis=0).astype(BF16)
+        high, low = split(lpad[...])
+        lmat[0:48] = dot(high, spread[0]).astype(BF16)
+        lmat[48:96] = dot(low, spread[1]).astype(BF16)
 
     def remap(index, c):
         if c:
@@ -331,12 +334,15 @@
         element, face = row & (wide - 1), row >> (7 if c == 1 else 8)
         tall = jnp.concatenate([us[c][q] for q in range(9)], axis=0)
         high = tall.astype(BF16).astype(F32)
-        both = jnp.concatenate([high, tall - high], axis=0).astype(BF16)
+        both = jnp.concatenate([high, tall - high], axis=1).astype(BF16)
         fill_one_hot(xtab, 0, [element], rows=wide)
-        picked = dot(both, xtab[0, 0:wide])
+        columns = xtab[0, 0:wide]
+        picked = dot(both, jnp.concatenate([columns, columns], axis=0))
         gap = jnp.zeros((8, 128), F32)
         for q in range(9):
-            pair = [picked[40 * q : 40 * q + 40], gap, picked[360 + 40 * q : 400 + 40 * q], gap]
+            x = picked[40 * q : 40 * q + 40]
+            high = x.astype(BF16).astype(F32)
+            pair = [high, gap, x - high, gap]
             stack3[q] = jnp.concatenate(pair, axis=0).astype(BF16)
         nodes = dot(emat[...], get(stack3))
         face = jnp.broadcast_to(face, (16, 128))
@@ -550,6 +556,7 @@
     hs2[0, 0] = sent2[:, 128:256]
     hs2[0, 1] = sent2[:, 0:128]
     start_halo(halo_c)
+    matrices()
     fetched(1, 2, 3, 7, 6, 13)
     coefficients(0)
     neighbour_table(0)

time: 33 us -> 32.9 us (level)
  no operation moved by 1% of the time
where the time goes in v6:
time: 32.9 us; the launch traced here: 32.8 us
  Pallas kernels  31.9 us (97%)
  local copies, waits for them, and re-layouts  0.87 us (3%)
    pallas_call x1, Pallas kernels, on_device(): pl.pallas_call(functools.partial(kernel, n_dom), out_shape=pltpu.VMEM(arr...  31.9 us
    unnamed x1, local copies, waits for them, and re-layouts  0.87 us

profile of v6, /device:TPU:512, one launch (start us, length us, event | category | flops | bytes accessed | tf_op | source)
XLA Modules:
  0.0 32.8 jit_solution(7398707813701252214)
XLA Ops:
  0.0 31.9 %step.1 = f32[9,35,448]{2,1,0:T(8,128)S(1)} custom-call(f32[9,35,448]{2,1,0:T(8,128)} %refs_0_.1, f32[3,448]{1,0:T(4,128)} %refs_1_.1, f32[3,3,448]{2,1,0:T(4,128)} %refs_2_.1, f32[4,448]{1,0:T(4,128)} %refs_3_.1, f32[3,35,35]{2,1,0:T(8,128)} %refs_4_.1, f32[35,60]{1,0:T(8,128)} %refs_5_.1, s32[4,448]{1,0:T(4,128)} %refs_6_.1, s32[4,448]{1,0:T(4,128)} %refs_7_.1, ...), custom_call_target="tpu_custom_call" | custom-call | tf_op jit(solution)/shard_map/step/pallas_call | solution.py:692
  31.9 0.9 %copy.16 = f32[9,35,448]{2,1,0:T(8,128)} copy(f32[9,35,448]{2,1,0:T(8,128)S(1)} %step.1) | data formatting | bytes 1128960
